TPU v7x, 256 devices: a whole 4x4x8 slice. The times are simulated.
256 devices in a mesh: chan: 32 (over x, z_hi, y), pos: 8 (over z_lo, core).
Axes of the slice: x: 4, y: 4, z: 8 (z_hi: 2, z_lo: 4; z = z_hi * 4 + z_lo), core: 2. Of those that a mesh axis runs over, the one named last changes fastest.
Arguments:
- patches: bfloat16 [32, 8, 512, 256], P(None, 'pos', 'chan'), may hold values from -30 to 30
- tok_weight: bfloat16 [32, 256, 1024], P('chan'), may hold values from -2 to 2
- mixing: bfloat16 [32, 16, 16], P('chan'), may hold values from -1.5 to 1.5
- chan_embed: bfloat16 [512, 1024], P('chan'), may hold values from -3 to 3
- norm_gain: float32 [1024], replicated, may hold values from 0.5 to 1.5
- qkv_weight: bfloat16 [1024, 3072], replicated, may hold values from -8 to 8
- upstream: bfloat16 [32, 8, 512, 1024], P(None, 'pos', 'chan'), may hold values from -6 to 6
Outputs:
- encoded: bfloat16 [32, 8, 512, 1024], P(None, 'pos', 'chan')
- tok_grad: float32 [8, 32, 256, 1024], P('pos', 'chan')
- mix_grad: float32 [32, 16, 16], P('chan')
- embed_grad: float32 [512, 1024], P('chan')
All inputs are finite; a program needn't handle non-finite values.
Results may differ from a plain program's by a relative error of at most 0.006.
The roundings to bfloat16 on the way count: a program that leaves them out, or rounds other values in their place, can miss the bound.
Values may be sent and summed in bfloat16 or wider, within the bound.
No kernel may reach another device: no remote copies, remote signals or barrier semaphores. Data moves between devices by JAX's collectives and lax.ppermute only.
A program may use at most 128 MiB of HBM per device.

v0:
```python
import math

import jax
import jax.numpy as jnp
from jax import lax
from jax.experimental import pallas as pl
from jax.experimental.pallas import tpu as pltpu
from jax.sharding import PartitionSpec as P


GROUP = 16
HEADS = 8
HDIM = 128
PAIR = 2 * HDIM
EPS = 1e-06
SCALE = 1.0 / math.sqrt(HDIM)
F32 = jnp.float32
BF16 = jnp.bfloat16


def nn(a, b):
    return jnp.dot(a, b, preferred_element_type=F32)


def nt(a, b):
    return lax.dot_general(a, b, (((1,), (1,)), ((), ())), preferred_element_type=F32)


def block_diagonal(small, size):
    rows = lax.broadcasted_iota(jnp.int32, (size, GROUP), 0)
    cols = lax.broadcasted_iota(jnp.int32, (size, GROUP), 1)
    pick = (rows % GROUP == cols).astype(BF16)
    tiled = nt(nn(pick, small).astype(BF16), pick)
    same = (
        lax.broadcasted_iota(jnp.int32, (size, size), 0) // GROUP
        == lax.broadcasted_iota(jnp.int32, (size, size), 1) // GROUP
    )
    return jnp.where(same, tiled, 0.0).astype(BF16), pick


def mix_kernel(patches_ref, weight_ref, mixing_ref, embed_ref, tokens_ref, mixed_ref):
    size = patches_ref.shape[0]
    tokens = nn(patches_ref[...], weight_ref[...]).astype(BF16)
    tokens_ref[...] = tokens
    diag, pick = block_diagonal(mixing_ref[...], size)
    mixed_ref[...] = (nn(diag, tokens) + nn(pick, embed_ref[...])).astype(BF16)


def forward_kernel(
    mixed_ref, gain_ref, wq_ref, wk_ref, wv_ref,
    encoded_ref, q_ref, k_ref, v_ref, probs_ref, inv_ref, normed_ref,
):
    step = pl.program_id(0)

    @pl.when(step == 0)
    def _():
        mixed = mixed_ref[...].reshape(normed_ref.shape).astype(F32)
        inv = lax.rsqrt(jnp.mean(mixed * mixed, axis=-1, keepdims=True) + EPS)
        inv_ref[...] = inv
        normed_ref[...] = (mixed * inv * gain_ref[...]).astype(BF16)

    normed = normed_ref[...]
    q_ref[...] = nn(normed, wq_ref[...]).astype(BF16)
    k_ref[...] = nn(normed, wk_ref[...]).astype(BF16)
    v_ref[...] = nn(normed, wv_ref[...]).astype(BF16)
    for i in range(2):
        cols = slice(i * HDIM, (i + 1) * HDIM)
        scores = nt(k_ref[:, cols], q_ref[:, cols]) * (SCALE * math.log2(math.e))
        exps = jnp.exp2(scores - jnp.max(scores, axis=0, keepdims=True))
        probs = exps * (1.0 / jnp.sum(exps, axis=0, keepdims=True))
        probs_ref[i] = probs
        attended = nn(v_ref[:, cols].T, probs.astype(BF16)).astype(BF16).T
        base = mixed_ref[:, :, pl.ds(pl.multiple_of(step * PAIR, PAIR) + i * HDIM, HDIM)]
        base = base.reshape(attended.shape)
        encoded_ref[:, cols] = (base.astype(F32) + attended.astype(F32)).astype(BF16)


def backward_kernel(
    upstream_ref, q_ref, k_ref, v_ref, probs_ref, wq_ref, wk_ref, wv_ref,
    mixed_ref, inv_ref, gain_ref, branch_ref, gq_ref, gk_ref, gv_ref, acc_ref,
):
    step = pl.program_id(0)
    for i in range(2):
        cols = slice(i * HDIM, (i + 1) * HDIM)
        up = upstream_ref[:, :, cols].reshape(-1, HDIM)
        probs = probs_ref[i]
        grad_probs = nt(v_ref[:, cols], up)
        inner = jnp.sum(probs * grad_probs, axis=0, keepdims=True)
        grad_scores = (probs * (grad_probs - inner) * SCALE).astype(BF16)
        gv_ref[:, cols] = nn(probs.astype(BF16), up).astype(BF16)
        gk_ref[:, cols] = nn(grad_scores, q_ref[:, cols]).astype(BF16)
        gq_ref[:, cols] = nn(k_ref[:, cols].T, grad_scores).astype(BF16).T
    grad = (
        nt(gq_ref[...], wq_ref[...]) + nt(gk_ref[...], wk_ref[...]) + nt(gv_ref[...], wv_ref[...])
    )

    @pl.when(step == 0)
    def _():
        acc_ref[...] = grad

    @pl.when(step > 0)
    def _():
        acc_ref[...] += grad

    @pl.when(step == pl.num_programs(0) - 1)
    def _():
        scaled = acc_ref[...] * gain_ref[...]
        mixed = mixed_ref[...].reshape(acc_ref.shape).astype(F32)
        inv = inv_ref[...]
        mean = jnp.mean(scaled * mixed, axis=-1, keepdims=True)
        branch_ref[...] = (inv * (scaled - mixed * (inv * inv * mean))).astype(BF16)


def partial_sums(rows_ref, tokens_ref):
    count = rows_ref.shape[0]
    width = rows_ref.shape[2]
    size = 256
    per = size // GROUP
    embed = jnp.sum(rows_ref[...].astype(F32), axis=0)
    folded = jnp.zeros((GROUP, size), F32)
    same = (
        lax.broadcasted_iota(jnp.int32, (size, size), 0) // GROUP
        == lax.broadcasted_iota(jnp.int32, (size, size), 1) // GROUP
    )
    for b in range(count // per):
        tokens = tokens_ref[b * size : (b + 1) * size, :]
        rows = rows_ref[b * per : (b + 1) * per].reshape(size, width)
        prods = jnp.where(same, nt(rows, tokens), 0.0)
        folded += jnp.sum(prods.reshape(per, GROUP, size), axis=0)
    folded = folded[:, :HDIM] + folded[:, HDIM:]
    for shift in (64, 32, 16):
        folded = folded + pltpu.roll(folded, shift, 1)
    return jnp.concatenate([embed, folded], axis=1)


def side_kernel(upstream_ref, tokens_ref, patches_ref, part_ref, pixels_ref):
    part_ref[...] = partial_sums(upstream_ref, tokens_ref)
    pixels_ref[...] = patches_ref[...].T


def sums_kernel(core_ref, part_ref, branch_ref, tokens_ref, keep_ref, send_ref):
    both = part_ref[...] + partial_sums(branch_ref, tokens_ref)
    half = GROUP // 2
    first = core_ref[0] == 0
    keep_ref[...] = jnp.where(first, both[:half], both[half:])
    send_ref[...] = jnp.where(first, both[half:], both[:half])


def weight_kernel(mixing_ref, upstream_ref, branch_ref, pixels_ref, out_ref):
    step = pl.program_id(0)
    size = pixels_ref.shape[1]
    width = upstream_ref.shape[2]
    diag, _ = block_diagonal(mixing_ref[...], size)
    up = upstream_ref[...].reshape(size, width)
    branch = branch_ref[...].reshape(size, width)
    diag_t = diag.T
    grad_tokens = (nn(diag_t, up) + nn(diag_t, branch)).astype(BF16)
    part = nn(pixels_ref[...], grad_tokens)

    @pl.when(step == 0)
    def _():
        out_ref[...] = part

    @pl.when(step > 0)
    def _():
        out_ref[...] += part


def final_kernel(core_ref, mine_ref, other_ref, embed_ref, mix_ref):
    half = GROUP // 2
    width = embed_ref.shape[1]
    first = core_ref[0] == 0
    mine = mine_ref[...]
    other = other_ref[...]
    low = jnp.where(first, mine, other)
    high = jnp.where(first, other, mine)
    embed_ref[:half, :] = low[:, :width]
    embed_ref[half:, :] = high[:, :width]
    mix_ref[:half, :] = low[:, width : width + GROUP]
    mix_ref[half:, :] = high[:, width : width + GROUP]


def to_hbm(x):
    return pltpu.with_memory_space_constraint(x, pltpu.HBM)


def whole(shape):
    return pl.BlockSpec(shape, lambda *_: (0,) * len(shape))


def shape(dims, dtype):
    return jax.ShapeDtypeStruct(dims, dtype)


def cost(flops, read):
    return pl.CostEstimate(flops=flops, bytes_accessed=read, transcendentals=0)


def step(patches, tok_weight, mixing, chan_embed, norm_gain, qkv_weight, upstream):
    count = patches.shape[0]
    pix = patches.shape[3]
    width = tok_weight.shape[2]
    rows = count * GROUP
    chans = lax.axis_size("chan") * GROUP
    steps = width // PAIR
    post = (chans // GROUP, GROUP, width)
    patches = patches.reshape(rows, pix)
    tok_weight = tok_weight.reshape(pix, width)
    mixing = mixing.reshape(GROUP, GROUP)
    upstream = upstream.reshape(count, GROUP, width)
    gain = norm_gain.reshape(1, width)
    block = 256
    tokens, mixed = pl.pallas_call(
        mix_kernel,
        grid=(rows // block,),
        in_specs=[
            pl.BlockSpec((block, pix), lambda i: (i, 0)),
            whole((pix, width)),
            whole((GROUP, GROUP)),
            whole((GROUP, width)),
        ],
        out_specs=[pl.BlockSpec((block, width), lambda i: (i, 0))] * 2,
        out_shape=[shape((rows, width), BF16)] * 2,
        cost_estimate=cost(4 * rows * pix * width, 4 * rows * width),
        name="mix",
    )(patches, tok_weight, mixing, chan_embed)

    def exchange(x):
        return lax.all_to_all(x.reshape(-1, GROUP, width), "chan", 0, 0, tiled=True)

    mixed_post = to_hbm(exchange(mixed))
    upstream_post = to_hbm(exchange(upstream))
    vmem = pl.BlockSpec(memory_space=pltpu.VMEM)
    part, pixels = pl.pallas_call(
        side_kernel,
        in_specs=[vmem] * 3,
        out_specs=[vmem] * 2,
        out_shape=[shape((GROUP, width + HDIM), F32), shape((pix, rows), BF16)],
        cost_estimate=cost(2 * rows * block * width, 4 << 20),
        name="side",
    )(upstream, tokens, patches)
    column = lambda part: pl.BlockSpec((width, PAIR), lambda i: (0, part * steps + i))
    heads = pl.BlockSpec((chans, PAIR), lambda i: (0, i))
    pairs = pl.BlockSpec((2, chans, chans), lambda i: (i, 0, 0))
    encoded, q, k, v, probs, inv = pl.pallas_call(
        forward_kernel,
        grid=(steps,),
        in_specs=[whole(post), whole((1, width)), column(0), column(1), column(2)],
        out_specs=[heads, heads, heads, heads, pairs, whole((chans, 1))],
        out_shape=[shape((chans, width), BF16)] * 4
        + [shape((HEADS, chans, chans), F32), shape((chans, 1), F32)],
        scratch_shapes=[pltpu.VMEM((chans, width), BF16)],
        cost_estimate=cost(6 * chans * width * width + 4 * chans * chans * width, 16 << 20),
        name="attend_forward",
    )(mixed_post, gain, qkv_weight, qkv_weight, qkv_weight)
    encoded = exchange(encoded)
    branch = pl.pallas_call(
        backward_kernel,
        grid=(steps,),
        in_specs=[pl.BlockSpec((*post[:2], PAIR), lambda i: (0, 0, i))]
        + [heads] * 3
        + [pairs, column(0), column(1), column(2)]
        + [whole(post), whole((chans, 1)), whole((1, width))],
        out_specs=whole((chans, width)),
        out_shape=shape((chans, width), BF16),
        scratch_shapes=[pltpu.VMEM((chans, PAIR), BF16)] * 3 + [pltpu.VMEM((chans, width), F32)],
        cost_estimate=cost(6 * chans * width * width + 8 * chans * chans * width, 16 << 20),
        name="attend_backward",
    )(upstream_post, q, k, v, probs, qkv_weight, qkv_weight, qkv_weight, mixed_post, inv, gain)
    branch = to_hbm(exchange(branch))
    core = (lax.axis_index("pos") % 2).astype(jnp.int32).reshape(1)
    smem = pl.BlockSpec(memory_space=pltpu.SMEM)
    half = shape((GROUP // 2, width + HDIM), F32)
    keep, send = pl.pallas_call(
        sums_kernel,
        in_specs=[smem] + [vmem] * 3,
        out_specs=[vmem] * 2,
        out_shape=[half] * 2,
        cost_estimate=cost(2 * rows * block * width, 4 << 20),
        name="sums",
    )(core, part, branch, tokens)
    ranks = range(lax.axis_size("pos"))

    def swap(x, bit):
        return lax.ppermute(x, "pos", [(p, p ^ bit) for p in ranks])

    total = keep + swap(send, 1)
    total = (total + swap(total, 2)) + (swap(total, 4) + swap(total, 6))
    embed_grad, mix_grad = pl.pallas_call(
        final_kernel,
        in_specs=[smem] + [vmem] * 2,
        out_specs=[vmem] * 2,
        out_shape=[shape((GROUP, width), F32), shape((GROUP, GROUP), F32)],
        name="final",
    )(core, total, swap(total, 1))
    per = block // GROUP
    tok_grad = pl.pallas_call(
        weight_kernel,
        grid=(rows // block,),
        in_specs=[
            whole((GROUP, GROUP)),
            pl.BlockSpec((per, GROUP, width), lambda i: (i, 0, 0)),
            pl.BlockSpec((per, GROUP, width), lambda i: (i, 0, 0)),
            pl.BlockSpec((pix, block), lambda i: (0, i)),
        ],
        out_specs=whole((pix, width)),
        out_shape=shape((pix, width), F32),
        cost_estimate=cost(8 * rows * pix * width, 4 << 20),
        name="weight",
    )
    tok_grad = tok_grad(mixing, upstream, branch, pixels)
    return (
        encoded.reshape(count, 1, GROUP, width),
        tok_grad.reshape(1, 1, pix, width),
        mix_grad.reshape(1, GROUP, GROUP),
        embed_grad,
    )


def solution(mesh):
    in_specs = (
        P(None, "pos", "chan", None),
        P("chan", None, None),
        P("chan", None, None),
        P("chan", None),
        P(),
        P(),
        P(None, "pos", "chan", None),
    )
    out_specs = (
        P(None, "pos", "chan", None),
        P("pos", "chan", None, None),
        P("chan", None, None),
        P("chan", None),
    )
    return jax.shard_map(step, mesh=mesh, in_specs=in_specs, out_specs=out_specs, check_vma=False)
```

profile of v0, /device:TPU:1, one launch (start us, length us, event | category | flops | bytes accessed | tf_op | source)
XLA Modules:
  0.0 164.4 jit_solution(4129330695686292757)
XLA Ops:
  0.6 3.5 %mix.1 = (bf16[512,1024]{1,0:T(8,128)(2,1)}, bf16[512,1024]{1,0:T(8,128)(2,1)}) custom-call(bf16[512,256]{1,0:T(8,128)(2,1)} %bitcast.18, bf16[256,1024]{1,0:T(8,128)(2,1)} %bitcast.22, bf16[16,16]{1,0:T(8,128)(2,1)} %bitcast.24, bf16[16,1024]{1,0:T(8,128)(2,1)} %embed_ref.1), custom_call_target="tpu_custom_call" | custom-call | flops 536870912 | bytes 2097152 | tf_op jit(solution)/shard_map/mix/pallas_call | solution.py:213
  4.1 36.5 %all_to_all.20.mixed_ref = bf16[32,16,1024]{2,1,0:T(8,128)(2,1)} all-to-all(bf16[32,16,1024]{2,1,0:T(8,128)(2,1)} %bitcast.17), channel_id=1, replica_groups=mesh['chan'=32,'pos'=8] {'chan'}, dimensions={0} | all-to-all | bytes 2097152 | tf_op jit(solution)/shard_map/all_to_all | solution.py:229
  40.6 4.3 %all-to-all-start.2 = ((bf16[32,16,1024]{2,1,0:T(8,128)(2,1)}), bf16[32,16,1024]{2,1,0:T(8,128)(2,1)S(1)}, u32[]{:S(2)}, u32[]{:S(2)}) async-start(bf16[32,16,1024]{2,1,0:T(8,128)(2,1)} %bitcast.13), calls=%async_computation.2 | async-start | bytes 2097152 | tf_op jit(solution)/shard_map/all_to_all | solution.py:229
  45.0 13.7 %attend_forward.1 = (bf16[512,1024]{1,0:T(8,128)(2,1)}, bf16[512,1024]{1,0:T(8,128)(2,1)}, bf16[512,1024]{1,0:T(8,128)(2,1)}, bf16[512,1024]{1,0:T(8,128)(2,1)},...) custom-call(bf16[32,16,1024]{2,1,0:T(8,128)(2,1)} %all_to_all.20.mixed_ref, f32[1,1024]{1,0:T(1,128)} %bitcast.20, ...), custom_call_target="tpu_custom_call" | custom-call | flops 4294967296 | bytes 16777216 | tf_op jit(solution)/shard_map/attend_forward/pallas_call | solution.py:245
  58.7 1.5 all-to-all-done.2.upstream_ref
  60.2 0.0 copy-start
  60.2 1.0 copy-done
  61.2 14.9 %attend_backward.1 = bf16[512,1024]{1,0:T(8,128)(2,1)} custom-call(bf16[32,16,1024]{2,1,0:T(8,128)(2,1)} %copy-done, bf16[512,1024]{1,0:T(8,128)(2,1)} %get-tuple-element.20.q_ref, bf16[512,1024]{1,0:T(8,128)(2,1)} %get-tuple-element.21.k_ref, bf16[512,1024]{1,0:T(8,128)(2,1)} %get-tuple-element.22.v_ref, f32[8,512,512]{2,1,0:T(8,128)} %get-tuple-element.23.probs_ref, ...), custom_call_target="tpu_custom_call" | custom-call | flops 5368709120 | bytes 16777216 | tf_op jit(solution)/shard_map/attend_backward/pallas_call | solution.py:257
  76.1 25.3 %all_to_all.21.branch_ref = bf16[32,16,1024]{2,1,0:T(8,128)(2,1)} all-to-all(bf16[32,16,1024]{2,1,0:T(8,128)(2,1)} %bitcast.12), channel_id=1, replica_groups=mesh['chan'=32,'pos'=8] {'chan'}, dimensions={0} | all-to-all | bytes 2097152 | tf_op jit(solution)/shard_map/all_to_all | solution.py:229
  101.3 4.5 %all-to-all-start.1 = ((bf16[32,16,1024]{2,1,0:T(8,128)(2,1)}), bf16[32,16,1024]{2,1,0:T(8,128)(2,1)S(1)}, u32[]{:S(2)}, u32[]{:S(2)}) async-start(bf16[32,16,1024]{2,1,0:T(8,128)(2,1)} %bitcast.5), calls=%async_computation.1 | async-start | bytes 2097152 | tf_op jit(solution)/shard_map/all_to_all | solution.py:229
  105.9 3.0 %side.1 = (f32[16,1152]{1,0:T(8,128)}, bf16[256,512]{1,0:T(8,128)(2,1)}) custom-call(bf16[32,16,1024]{2,1,0:T(8,128)(2,1)} %bitcast.14, bf16[512,1024]{1,0:T(8,128)(2,1)} %get-tuple-element.25.tokens_ref, bf16[512,256]{1,0:T(8,128)(2,1)} %bitcast.19), custom_call_target="tpu_custom_call" | custom-call | flops 268435456 | bytes 4194304 | tf_op jit(solution)/shard_map/side/pallas_call | solution.py:234
  108.9 2.9 %sums.1 = (f32[8,1152]{1,0:T(8,128)}, f32[8,1152]{1,0:T(8,128)}) custom-call(s32[1]{0:T(128)} %bitcast.10.core_ref, f32[16,1152]{1,0:T(8,128)} %get-tuple-element.27.part_ref, bf16[32,16,1024]{2,1,0:T(8,128)(2,1)} %all_to_all.21.branch_ref, bf16[512,1024]{1,0:T(8,128)(2,1)} %get-tuple-element.25.tokens_ref), custom_call_target="tpu_custom_call" | custom-call | flops 268435456 | bytes 4194304 | tf_op jit(solution)/shard_map/sums/pallas_call | solution.py:274
  111.9 14.1 %collective-permute-start = (f32[8,1152]{1,0:T(8,128)}, f32[8,1152]{1,0:T(8,128)S(1)}, u32[]{:S(2)}, u32[]{:S(2)}) collective-permute-start(f32[8,1152]{1,0:T(8,128)} %get-tuple-element.29), channel_id=1, source_target_pairs={{0,1},{1,0},{2,3},{3,2},{4,5},{5,4},{6,7},{7,6},{8,9},{9,8},{10,11... | collective-permute-start | bytes 110600 | tf_op jit(solution)/shard_map/ppermute | solution.py:285
  126.0 1.1 collective-permute-done
  127.1 0.8 add.17
  127.8 18.3 %collective-permute-start.2 = (f32[8,1152]{1,0:T(8,128)S(1)}, f32[8,1152]{1,0:T(8,128)S(1)}, u32[]{:S(2)}, u32[]{:S(2)}) collective-permute-start(f32[8,1152]{1,0:T(8,128)S(1)} %add.17), channel_id=1, source_target_pairs={{0,4},{1,5},{2,6},{3,7},{4,0},{5,1},{6,2},{7,3},{8,12},{9,13},{10,... | collective-permute-start | bytes 110600 | tf_op jit(solution)/shard_map/ppermute | solution.py:285
  146.2 1.6 collective-permute-start.3
  147.8 0.0 collective-permute-start.1
  147.8 8.7 %collective-permute-done.2 = f32[8,1152]{1,0:T(8,128)S(1)} collective-permute-done((f32[8,1152]{1,0:T(8,128)S(1)}, f32[8,1152]{1,0:T(8,128)S(1)}, u32[]{:S(2)}, u32[]{:S(2)}) %collective-permute-start.2) | collective-permute-done | bytes 36896 | tf_op jit(solution)/shard_map/ppermute | solution.py:285
  156.5 0.0 collective-permute-done.3
  156.5 0.0 collective-permute-done.1
  156.6 0.0 copy-start.1
  156.6 0.6 collective-permute-start.4
  157.1 4.2 %weight.1 = f32[256,1024]{1,0:T(8,128)} custom-call(bf16[16,16]{1,0:T(8,128)(2,1)} %bitcast.25, bf16[32,16,1024]{2,1,0:T(8,128)(2,1)} %bitcast.15, bf16[32,16,1024]{2,1,0:T(8,128)(2,1)} %all_to_all.21.branch_ref, bf16[256,512]{1,0:T(8,128)(2,1)} %get-tuple-element.26.pixels_ref), custom_call_target="tpu_custom_call" | custom-call | flops 1073741824 | bytes 4194304 | tf_op jit(solution)/shard_map/weight/pallas_call | solution.py:311
  161.4 0.0 all-to-all-done.1
  161.4 0.0 collective-permute-done.4.other_ref
  161.4 0.0 copy-done.1
  161.4 0.0 copy-start.2
  161.4 0.6 copy-done.2
  162.0 1.4 final.1
  163.5 1.0 copy.12
  (1 shorter events, 0.0 us)
Async XLA Ops:
  40.6 19.6 %all-to-all-start.2 = ((bf16[32,16,1024]{2,1,0:T(8,128)(2,1)}), bf16[32,16,1024]{2,1,0:T(8,128)(2,1)S(1)}, u32[]{:S(2)}, u32[]{:S(2)}) async-start(bf16[32,16,1024]{2,1,0:T(8,128)(2,1)} %bitcast.13), calls=%async_computation.2 | async-start | bytes 2097152 | tf_op jit(solution)/shard_map/all_to_all | solution.py:229
  60.2 1.0 copy-start
  101.3 60.0 %all-to-all-start.1 = ((bf16[32,16,1024]{2,1,0:T(8,128)(2,1)}), bf16[32,16,1024]{2,1,0:T(8,128)(2,1)S(1)}, u32[]{:S(2)}, u32[]{:S(2)}) async-start(bf16[32,16,1024]{2,1,0:T(8,128)(2,1)} %bitcast.5), calls=%async_computation.1 | async-start | bytes 2097152 | tf_op jit(solution)/shard_map/all_to_all | solution.py:229
  111.9 15.2 %collective-permute-start = (f32[8,1152]{1,0:T(8,128)}, f32[8,1152]{1,0:T(8,128)S(1)}, u32[]{:S(2)}, u32[]{:S(2)}) collective-permute-start(f32[8,1152]{1,0:T(8,128)} %get-tuple-element.29), channel_id=1, source_target_pairs={{0,1},{1,0},{2,3},{3,2},{4,5},{5,4},{6,7},{7,6},{8,9},{9,8},{10,11... | collective-permute-start | bytes 110600 | tf_op jit(solution)/shard_map/ppermute | solution.py:285
  127.8 28.7 %collective-permute-start.2 = (f32[8,1152]{1,0:T(8,128)S(1)}, f32[8,1152]{1,0:T(8,128)S(1)}, u32[]{:S(2)}, u32[]{:S(2)}) collective-permute-start(f32[8,1152]{1,0:T(8,128)S(1)} %add.17), channel_id=1, source_target_pairs={{0,4},{1,5},{2,6},{3,7},{4,0},{5,1},{6,2},{7,3},{8,12},{9,13},{10,... | collective-permute-start | bytes 110600 | tf_op jit(solution)/shard_map/ppermute | solution.py:285
  146.2 10.4 %collective-permute-start.3 = (f32[8,1152]{1,0:T(8,128)S(1)}, f32[8,1152]{1,0:T(8,128)S(1)}, u32[]{:S(2)}, u32[]{:S(2)}) collective-permute-start(f32[8,1152]{1,0:T(8,128)S(1)} %add.17), channel_id=1, source_target_pairs={{0,6},{1,7},{2,4},{3,5},{4,2},{5,3},{6,0},{7,1},{8,14},{9,15},{10,... | collective-permute-start | bytes 110600 | tf_op jit(solution)/shard_map/ppermute | solution.py:285
  147.8 8.8 %collective-permute-start.1 = (f32[8,1152]{1,0:T(8,128)S(1)}, f32[8,1152]{1,0:T(8,128)S(1)}, u32[]{:S(2)}, u32[]{:S(2)}) collective-permute-start(f32[8,1152]{1,0:T(8,128)S(1)} %add.17), channel_id=1, source_target_pairs={{0,2},{1,3},{2,0},{3,1},{4,6},{5,7},{6,4},{7,5},{8,10},{9,11},{10,... | collective-permute-start | bytes 110600 | tf_op jit(solution)/shard_map/ppermute | solution.py:285
  156.6 4.8 %copy-start.1 = (f32[8,1152]{1,0:T(8,128)}, f32[8,1152]{1,0:T(8,128)S(1)}, u32[]{:S(2)}) copy-start(f32[8,1152]{1,0:T(8,128)S(1)} %add_add_fusion.mine_ref) | copy-start | bytes 110596
  156.6 4.8 %collective-permute-start.4 = (f32[8,1152]{1,0:T(8,128)S(1)}, f32[8,1152]{1,0:T(8,128)S(1)}, u32[]{:S(2)}, u32[]{:S(2)}) collective-permute-start(f32[8,1152]{1,0:T(8,128)S(1)} %add_add_fusion.mine_ref), channel_id=1, source_target_pairs={{0,1},{1,0},{2,3},{3,2},{4,5},{5,4},{6,7},{7,6},{8,9},{9,8},{10,11... | collective-permute-start | bytes 110600 | tf_op jit(solution)/shard_map/ppermute | solution.py:285
  161.4 0.6 copy-start.2
where the time goes:
time: 165 us; the launch traced here: 164 us
  blocking collectives  61.8 us (37%)
  Pallas kernels  43.8 us (27%)
  starting transfers between devices  43.5 us (26%)
  waiting for transfers between devices  11.4 us (7%)
  local copies, waits for them, and re-layouts  2.55 us (2%)
    all_to_all x2, blocking collectives, exchange(): return lax.all_to_all(x.reshape(-1, GROUP, width), 'chan', 0, 0, tiled=True)  61.8 us
    ppermute x5, starting transfers between devices, swap(): return lax.ppermute(x, 'pos', [(p, p ^ bit) for p in ranks])  34.6 us
    pallas_call x1, Pallas kernels, step(): pl.pallas_call(backward_kernel, grid=(steps,), in_specs=[pl.BlockSpec((*p...  14.9 us
    pallas_call x1, Pallas kernels, step(): pl.pallas_call(forward_kernel, grid=(steps,), in_specs=[whole(post), whol...  13.7 us
    ppermute x5, waiting for transfers between devices, swap(): return lax.ppermute(x, 'pos', [(p, p ^ bit) for p in ranks])  9.83 us
    all_to_all x2, starting transfers between devices, exchange(): return lax.all_to_all(x.reshape(-1, GROUP, width), 'chan', 0, 0, tiled=True)  8.83 us
    pallas_call x1, Pallas kernels, step(): tok_grad = tok_grad(mixing, upstream, branch, pixels)  4.25 us
    pallas_call x1, Pallas kernels, step(): pl.pallas_call(mix_kernel, grid=(rows // block,), in_specs=[pl.BlockSpec(...  3.51 us
  transfers between devices with their start and end apart: 7, of which 3 were waited for; matrix products, arithmetic and copies ran while one was open for 0% of the time, Pallas kernels for 15%

commit v1 on v0

v1 whole, which is shorter than its diff:
```python
import math

import jax
import jax.numpy as jnp
from jax import lax
from jax.experimental import pallas as pl
from jax.experimental.pallas import tpu as pltpu
from jax.sharding import PartitionSpec as P


GROUP = 16
HEADS = 8
HDIM = 128
PAIR = 2 * HDIM
EPS = 1e-06
SCALE = 1.0 / math.sqrt(HDIM)
X, HALVES, Y = 4, 2, 4
PLANE = X * Y
BASE = [x * HALVES * Y + y for x in range(X) for y in range(Y)]
F32 = jnp.float32
BF16 = jnp.bfloat16


def nn(a, b):
    return jnp.dot(a, b, preferred_element_type=F32)


def nt(a, b):
    return lax.dot_general(a, b, (((1,), (1,)), ((), ())), preferred_element_type=F32)


def block_diagonal(small, size):
    rows = lax.broadcasted_iota(jnp.int32, (size, GROUP), 0)
    cols = lax.broadcasted_iota(jnp.int32, (size, GROUP), 1)
    pick = (rows % GROUP == cols).astype(BF16)
    tiled = nt(nn(pick, small).astype(BF16), pick)
    same = (
        lax.broadcasted_iota(jnp.int32, (size, size), 0) // GROUP
        == lax.broadcasted_iota(jnp.int32, (size, size), 1) // GROUP
    )
    return jnp.where(same, tiled, 0.0).astype(BF16), pick


def mix_block(start, patches_ref, weight_ref, mixing_ref, embed_ref, tokens_ref):
    pixels = jnp.concatenate([patches_ref[base + start] for base in BASE], axis=0)
    tokens = nn(pixels, weight_ref[...]).astype(BF16)
    tokens_ref[...] = tokens
    diag, pick = block_diagonal(mixing_ref[...], tokens.shape[0])
    mixed = (nn(diag, tokens) + nn(pick, embed_ref[...])).astype(BF16)
    return mixed.reshape(PLANE, GROUP, -1)


def mix_kernel(start_ref, patches_ref, weight_ref, mixing_ref, embed_ref, tokens_ref, mixed_ref):
    mixed_ref[...] = mix_block(
        start_ref[0], patches_ref, weight_ref, mixing_ref, embed_ref, tokens_ref
    )


def mix_near_kernel(
    start_ref, patches_ref, weight_ref, mixing_ref, embed_ref, upstream_ref, tokens_ref, both_ref
):
    both_ref[:, :GROUP] = mix_block(
        start_ref[0], patches_ref, weight_ref, mixing_ref, embed_ref, tokens_ref
    )
    both_ref[:, GROUP:] = upstream_ref[...]


def pack_kernel(same_ref, other_ref, both_ref):
    both_ref[:, :GROUP] = same_ref[...]
    both_ref[:, GROUP:] = other_ref[...]


def split_kernel(same_at, other_at, upstream_ref, same_ref, other_ref):
    for k, base in enumerate(BASE):
        same_ref[k] = upstream_ref[base + same_at[0]]
        other_ref[k] = upstream_ref[base + other_at[0]]


def place_kernel(same_at, other_at, both_ref, out_ref):
    for k, base in enumerate(BASE):
        out_ref[base + same_at[0]] = both_ref[k, :GROUP]
        out_ref[base + other_at[0]] = both_ref[k, GROUP:]


def project_kernel(
    near_ref, far_ref, gain_ref, wq_ref, wk_ref, wv_ref, q_ref, k_ref, v_ref, inv_ref, normed_ref
):
    half = normed_ref.shape[0] // 2

    @pl.when(pl.program_id(0) == 0)
    def _():
        for ref, at in ((near_ref, 0), (far_ref, half)):
            mixed = ref[:, :GROUP].reshape(half, -1).astype(F32)
            inv = lax.rsqrt(jnp.mean(mixed * mixed, axis=-1, keepdims=True) + EPS)
            inv_ref[at : at + half] = inv
            normed_ref[at : at + half] = (mixed * inv * gain_ref[...]).astype(BF16)

    normed = normed_ref[...]
    q_ref[...] = nn(normed, wq_ref[...]).astype(BF16)
    k_ref[...] = nn(normed, wk_ref[...]).astype(BF16)
    v_ref[...] = nn(normed, wv_ref[...]).astype(BF16)


def forward_kernel(near_ref, far_ref, q_ref, k_ref, v_ref, first_ref, second_ref, probs_ref):
    step = pl.program_id(0)
    half = first_ref.shape[0]
    for i in range(2):
        cols = slice(i * HDIM, (i + 1) * HDIM)
        scores = nt(k_ref[:, cols], q_ref[:, cols]) * (SCALE * math.log2(math.e))
        exps = jnp.exp2(scores - jnp.max(scores, axis=0, keepdims=True))
        probs = exps * (1.0 / jnp.sum(exps, axis=0, keepdims=True))
        probs_ref[i] = probs
        attended = nn(v_ref[:, cols].T, probs.astype(BF16)).astype(BF16).T
        here = pl.ds(pl.multiple_of(step * PAIR, PAIR) + i * HDIM, HDIM)
        for ref, out_ref, at in ((near_ref, first_ref, 0), (far_ref, second_ref, half)):
            base = ref[:, :GROUP, here].reshape(half, HDIM).astype(F32)
            out_ref[:, cols] = (base + attended[at : at + half].astype(F32)).astype(BF16)


def backward_kernel(
    near_at, far_at,
    near_ref, up_far_ref, q_ref, k_ref, v_ref, probs_ref, wq_ref, wk_ref, wv_ref,
    far_ref, inv_ref, gain_ref, branch_ref, gq_ref, gk_ref, gv_ref, acc_ref,
):
    step = pl.program_id(0)
    half = acc_ref.shape[0] // 2
    for i in range(2):
        cols = slice(i * HDIM, (i + 1) * HDIM)
        here = pl.ds(pl.multiple_of(step * PAIR, PAIR) + i * HDIM, HDIM)
        up = jnp.concatenate(
            [
                near_ref[:, GROUP:, here].reshape(half, HDIM),
                up_far_ref[:, :, here].reshape(half, HDIM),
            ],
            axis=0,
        )
        probs = probs_ref[i]
        grad_probs = nt(v_ref[:, cols], up)
        inner = jnp.sum(probs * grad_probs, axis=0, keepdims=True)
        grad_scores = (probs * (grad_probs - inner) * SCALE).astype(BF16)
        gv_ref[:, cols] = nn(probs.astype(BF16), up).astype(BF16)
        gk_ref[:, cols] = nn(grad_scores, q_ref[:, cols]).astype(BF16)
        gq_ref[:, cols] = nn(k_ref[:, cols].T, grad_scores).astype(BF16).T
    grad = (
        nt(gq_ref[...], wq_ref[...]) + nt(gk_ref[...], wk_ref[...]) + nt(gv_ref[...], wv_ref[...])
    )

    @pl.when(step == 0)
    def _():
        acc_ref[...] = grad

    @pl.when(step > 0)
    def _():
        acc_ref[...] += grad

    @pl.when(step == pl.num_programs(0) - 1)
    def _():
        for ref, to, at in ((near_ref, near_at, 0), (far_ref, far_at, half)):
            scaled = acc_ref[at : at + half] * gain_ref[...]
            mixed = ref[:, :GROUP].reshape(half, -1).astype(F32)
            inv = inv_ref[at : at + half]
            mean = jnp.mean(scaled * mixed, axis=-1, keepdims=True)
            branch = (inv * (scaled - mixed * (inv * inv * mean))).astype(BF16)
            branch_ref[pl.ds(to[0], PLANE)] = branch.reshape(PLANE, GROUP, -1)


def partial_sums(rows, tokens):
    count, _, width = rows.shape
    size = count * GROUP
    embed = jnp.sum(rows.astype(F32), axis=0)
    same = (
        lax.broadcasted_iota(jnp.int32, (size, size), 0) // GROUP
        == lax.broadcasted_iota(jnp.int32, (size, size), 1) // GROUP
    )
    prods = jnp.where(same, nt(rows.reshape(size, width), tokens), 0.0)
    folded = jnp.sum(prods.reshape(count, GROUP, size), axis=0)
    folded = folded[:, :HDIM] + folded[:, HDIM:]
    for shift in (64, 32, 16):
        folded = folded + pltpu.roll(folded, shift, 1)
    return jnp.concatenate([embed, folded], axis=1)


def side_kernel(
    same_at, other_at, up_same_ref, up_other_ref, tok_same_ref, tok_other_ref, patches_ref,
    part_ref, pix_same_ref, pix_other_ref, tokens_ref,
):
    tokens_ref[: tok_same_ref.shape[0]] = tok_same_ref[...]
    tokens_ref[tok_same_ref.shape[0] :] = tok_other_ref[...]
    part_ref[...] = partial_sums(up_same_ref[...], tok_same_ref[...]) + partial_sums(
        up_other_ref[...], tok_other_ref[...]
    )
    for at, pixels_ref in ((same_at, pix_same_ref), (other_at, pix_other_ref)):
        start = at[0]
        pixels_ref[...] = jnp.concatenate([patches_ref[base + start] for base in BASE], axis=0).T


def sums_kernel(
    core_ref, near_at, far_at, part_ref, branch_ref, tokens_ref, keep_ref, send_ref
):
    both = part_ref[...]
    size = PLANE * GROUP
    for i, at in enumerate((near_at, far_at)):
        tokens = tokens_ref[i * size : (i + 1) * size]
        both += partial_sums(branch_ref[pl.ds(at[0], PLANE)], tokens)
    half = GROUP // 2
    first = core_ref[0] == 0
    keep_ref[...] = jnp.where(first, both[:half], both[half:])
    send_ref[...] = jnp.where(first, both[half:], both[:half])


def weight_kernel(
    near_at, far_at, mixing_ref, up_same_ref, up_other_ref, branch_ref, pix_same_ref,
    pix_other_ref, out_ref,
):
    size = pix_same_ref.shape[1]
    width = out_ref.shape[1]
    diag, _ = block_diagonal(mixing_ref[...], size)
    diag_t = diag.T
    total = None
    for at, up_ref, pixels_ref in (
        (near_at, up_same_ref, pix_same_ref), (far_at, up_other_ref, pix_other_ref)
    ):
        up = up_ref[...].reshape(size, width)
        branch = branch_ref[pl.ds(at[0], PLANE)].reshape(size, width)
        grad_tokens = (nn(diag_t, up) + nn(diag_t, branch)).astype(BF16)
        part = nn(pixels_ref[...], grad_tokens)
        total = part if total is None else total + part
    out_ref[...] = total


def final_kernel(core_ref, mine_ref, other_ref, embed_ref, mix_ref):
    half = GROUP // 2
    width = embed_ref.shape[1]
    first = core_ref[0] == 0
    mine = mine_ref[...]
    other = other_ref[...]
    low = jnp.where(first, mine, other)
    high = jnp.where(first, other, mine)
    embed_ref[:half, :] = low[:, :width]
    embed_ref[half:, :] = high[:, :width]
    mix_ref[:half, :] = low[:, width : width + GROUP]
    mix_ref[half:, :] = high[:, width : width + GROUP]


def to_vmem(x):
    return pltpu.with_memory_space_constraint(x, pltpu.VMEM)


def whole(shape):
    return pl.BlockSpec(shape, lambda *_: (0,) * len(shape))


def shape(dims, dtype):
    return jax.ShapeDtypeStruct(dims, dtype)


def cost(flops, read):
    return pl.CostEstimate(flops=flops, bytes_accessed=read, transcendentals=0)


def step(patches, tok_weight, mixing, chan_embed, norm_gain, qkv_weight, upstream):
    count = patches.shape[0]
    pix = patches.shape[3]
    width = tok_weight.shape[2]
    rows = PLANE * GROUP
    chans = lax.axis_size("chan") * GROUP
    steps = width // PAIR
    patches = patches.reshape(count, GROUP, pix)
    tok_weight = tok_weight.reshape(pix, width)
    mixing = mixing.reshape(GROUP, GROUP)
    upstream = upstream.reshape(count, GROUP, width)
    gain = norm_gain.reshape(1, width)
    vmem = pl.BlockSpec(memory_space=pltpu.VMEM)
    smem = pl.BlockSpec(memory_space=pltpu.SMEM)
    near = ((lax.axis_index("chan") // Y) % HALVES * Y).astype(jnp.int32).reshape(1)
    far = Y - near
    plane = [[base + h * Y for base in BASE] for h in range(HALVES)]
    piece = shape((PLANE, GROUP, width), BF16)

    def spread(x):
        x = x.reshape(PLANE, -1, width)
        return lax.all_to_all(x, "chan", 0, 0, axis_index_groups=plane, tiled=True)

    def flip(x):
        pairs = [(c, c ^ Y) for c in range(lax.axis_size("chan"))]
        return lax.ppermute(x.reshape(PLANE, GROUP, width), "chan", pairs)

    near_rank, far_rank = near // Y * PLANE, far // Y * PLANE

    tok_other, mixed_far = pl.pallas_call(
        mix_kernel,
        in_specs=[smem] + [vmem] * 4,
        out_specs=[vmem] * 2,
        out_shape=[shape((rows, width), BF16), piece],
        cost_estimate=cost(4 * rows * pix * width, 4 * rows * width),
        name="mix_other",
    )(far, patches, tok_weight, mixing, chan_embed)
    mixed_far = flip(mixed_far)
    up_same, up_other = pl.pallas_call(
        split_kernel,
        in_specs=[smem] * 2 + [vmem],
        out_specs=[vmem] * 2,
        out_shape=[piece] * 2,
        cost_estimate=cost(0, 4 << 20),
        name="split",
    )(near, far, upstream)
    up_far = flip(up_other)
    double = shape((PLANE, 2 * GROUP, width), BF16)
    tok_same, both = pl.pallas_call(
        mix_near_kernel,
        in_specs=[smem] + [vmem] * 5,
        out_specs=[vmem] * 2,
        out_shape=[shape((rows, width), BF16), double],
        cost_estimate=cost(4 * rows * pix * width, 4 * rows * width),
        name="mix_same",
    )(near, patches, tok_weight, mixing, chan_embed, up_same)
    both = spread(both)
    part, pix_same, pix_other, tokens = pl.pallas_call(
        side_kernel,
        in_specs=[smem] * 2 + [vmem] * 5,
        out_specs=[vmem] * 4,
        out_shape=[shape((GROUP, width + HDIM), F32)]
        + [shape((pix, rows), BF16)] * 2
        + [shape((chans, width), BF16)],
        cost_estimate=cost(4 * rows * rows * width, 4 << 20),
        name="side",
    )(near, far, up_same, up_other, tok_same, tok_other, patches)
    mixed_far = spread(mixed_far)
    column = lambda part: pl.BlockSpec((width, PAIR), lambda i: (0, part * steps + i))
    heads = pl.BlockSpec((chans, PAIR), lambda i: (0, i))
    half_heads = pl.BlockSpec((rows, PAIR), lambda i: (0, i))
    pairs = pl.BlockSpec((2, chans, chans), lambda i: (i, 0, 0))
    q, k, v, inv = pl.pallas_call(
        project_kernel,
        grid=(steps,),
        in_specs=[vmem, vmem, whole((1, width)), column(0), column(1), column(2)],
        out_specs=[heads, heads, heads, whole((chans, 1))],
        out_shape=[shape((chans, width), BF16)] * 3 + [shape((chans, 1), F32)],
        scratch_shapes=[pltpu.VMEM((chans, width), BF16)],
        cost_estimate=cost(6 * chans * width * width, 10 << 20),
        name="attend_project",
    )(to_vmem(both), to_vmem(mixed_far), gain, qkv_weight, qkv_weight, qkv_weight)
    up_far = spread(up_far)
    enc_same, enc_other, probs = pl.pallas_call(
        forward_kernel,
        grid=(steps,),
        in_specs=[vmem, vmem, heads, heads, heads],
        out_specs=[half_heads, half_heads, pairs],
        out_shape=[shape((rows, width), BF16)] * 2 + [shape((HEADS, chans, chans), F32)],
        cost_estimate=cost(4 * chans * chans * width, 14 << 20),
        name="attend_forward",
    )(to_vmem(both), to_vmem(mixed_far), q, k, v)
    enc_far = flip(enc_other)
    branch = pl.pallas_call(
        backward_kernel,
        grid=(steps,),
        in_specs=[smem] * 2
        + [vmem, vmem]
        + [heads] * 3
        + [pairs, column(0), column(1), column(2), vmem]
        + [whole((chans, 1)), whole((1, width))],
        out_specs=whole((count, GROUP, width)),
        out_shape=shape((count, GROUP, width), BF16),
        scratch_shapes=[pltpu.VMEM((chans, PAIR), BF16)] * 3 + [pltpu.VMEM((chans, width), F32)],
        cost_estimate=cost(6 * chans * width * width + 8 * chans * chans * width, 16 << 20),
        name="attend_backward",
    )(
        near_rank, far_rank, to_vmem(both), to_vmem(up_far), q, k, v, probs,
        qkv_weight, qkv_weight, qkv_weight, to_vmem(mixed_far), inv, gain,
    )
    order = [c for half in plane for c in half]
    branch = lax.all_to_all(branch, "chan", 0, 0, axis_index_groups=[order], tiled=True)
    encoded = pl.pallas_call(
        pack_kernel,
        in_specs=[vmem] * 2,
        out_specs=vmem,
        out_shape=double,
        cost_estimate=cost(0, 4 << 20),
        name="pack",
    )(enc_same.reshape(piece.shape), enc_far)
    encoded = spread(encoded)
    core = (lax.axis_index("pos") % 2).astype(jnp.int32).reshape(1)
    half = shape((GROUP // 2, width + HDIM), F32)
    keep, send = pl.pallas_call(
        sums_kernel,
        in_specs=[smem] * 3 + [vmem] * 3,
        out_specs=[vmem] * 2,
        out_shape=[half] * 2,
        cost_estimate=cost(2 * rows * rows * width, 4 << 20),
        name="sums",
    )(core, near_rank, far_rank, to_vmem(part), to_vmem(branch), tokens)
    ranks = range(lax.axis_size("pos"))

    def swap(x, bit):
        return lax.ppermute(x, "pos", [(p, p ^ bit) for p in ranks])

    total = keep + swap(send, 1)
    total = (total + swap(total, 2)) + (swap(total, 4) + swap(total, 6))
    embed_grad, mix_grad = pl.pallas_call(
        final_kernel,
        in_specs=[smem] + [vmem] * 2,
        out_specs=[vmem] * 2,
        out_shape=[shape((GROUP, width), F32), shape((GROUP, GROUP), F32)],
        name="final",
    )(core, to_vmem(total), to_vmem(swap(total, 1)))
    tok_grad = pl.pallas_call(
        weight_kernel,
        in_specs=[smem] * 2 + [vmem] * 6,
        out_specs=vmem,
        out_shape=shape((pix, width), F32),
        cost_estimate=cost(8 * rows * pix * width, 4 << 20),
        name="weight",
    )(near_rank, far_rank, mixing, up_same, up_other, branch, pix_same, pix_other)
    encoded = pl.pallas_call(
        place_kernel,
        in_specs=[smem] * 2 + [vmem],
        out_specs=vmem,
        out_shape=shape((count, GROUP, width), BF16),
        cost_estimate=cost(0, 4 << 20),
        name="place",
    )(near, far, to_vmem(encoded))
    return (
        encoded.reshape(count, 1, GROUP, width),
        tok_grad.reshape(1, 1, pix, width),
        mix_grad.reshape(1, GROUP, GROUP),
        embed_grad,
    )


def solution(mesh):
    in_specs = (
        P(None, "pos", "chan", None),
        P("chan", None, None),
        P("chan", None, None),
        P("chan", None),
        P(),
        P(),
        P(None, "pos", "chan", None),
    )
    out_specs = (
        P(None, "pos", "chan", None),
        P("pos", "chan", None, None),
        P("chan", None, None),
        P("chan", None),
    )
    return jax.shard_map(step, mesh=mesh, in_specs=in_specs, out_specs=out_specs, check_vma=False)
```

time: 165 us -> 198 us (1.20)
  blocking collectives: 61.8 us -> 0 us
  starting transfers between devices: 43.5 us -> 101 us
  waiting for transfers between devices: 11.4 us -> 38.4 us
  Pallas kernels: 43.8 us -> 53.1 us
    all_to_all x2 -> x0, blocking collectives: 61.8 us -> none  [exchange(): return lax.all_to_all(x.reshape(-1, GROUP, width), 'chan', 0, 0, tiled=True)]
    ppermute x0 -> x3, waiting for transfers between devices: none -> 34.7 us  [flip(): return lax.ppermute(x.reshape(PLANE, GROUP, width), 'chan', pairs)]
    all_to_all x2 -> x5, starting transfers between devices: 8.83 us -> 38.3 us  [the longest x4 26.4 us: spread(): return lax.all_to_all(x, 'chan', 0, 0, axis_index_groups=plane, tiled=True)]
    ppermute x5, starting transfers between devices: 34.6 us -> 51 us  [swap(): return lax.ppermute(x, 'pos', [(p, p ^ bit) for p in ranks])]
    ppermute x0 -> x3, starting transfers between devices: none -> 12.2 us  [flip(): return lax.ppermute(x.reshape(PLANE, GROUP, width), 'chan', pairs)]
    pallas_call x6 -> x11, Pallas kernels: 42.4 us -> 52.5 us  [the longest x1 15 us: step(): pl.pallas_call(backward_kernel, grid=(steps,), in_specs=[smem] * 2 + [vme...]
    ppermute x5, waiting for transfers between devices: 9.83 us -> 3.25 us  [swap(): return lax.ppermute(x, 'pos', [(p, p ^ bit) for p in ranks])]
  transfers between devices with their start and end apart: 7 -> 13, of which waited for: 3 -> 7; matrix products, arithmetic and copies ran while one was open for 0% -> 0% of each run, Pallas kernels for 15% -> 16%
where the time goes in v1:
time: 198 us; the launch traced here: 196 us
  starting transfers between devices  101 us (51%)
  Pallas kernels  53.1 us (27%)
  waiting for transfers between devices  38.4 us (19%)
    ppermute x5, starting transfers between devices, swap(): return lax.ppermute(x, 'pos', [(p, p ^ bit) for p in ranks])  51 us
    ppermute x3, waiting for transfers between devices, flip(): return lax.ppermute(x.reshape(PLANE, GROUP, width), 'chan', pairs)  34.7 us
    all_to_all x4, starting transfers between devices, spread(): return lax.all_to_all(x, 'chan', 0, 0, axis_index_groups=plane, tiled=True)  26.4 us
    pallas_call x1, Pallas kernels, step(): pl.pallas_call(backward_kernel, grid=(steps,), in_specs=[smem] * 2 + [vme...  15 us
    ppermute x3, starting transfers between devices, flip(): return lax.ppermute(x.reshape(PLANE, GROUP, width), 'chan', pairs)  12.2 us
    all_to_all x1, starting transfers between devices, step(): lax.all_to_all(branch, 'chan', 0, 0, axis_index_groups=[order], tiled=True)  11.9 us
    pallas_call x1, Pallas kernels, step(): pl.pallas_call(forward_kernel, grid=(steps,), in_specs=[vmem, vmem, heads...  8.93 us
    pallas_call x1, Pallas kernels, step(): pl.pallas_call(project_kernel, grid=(steps,), in_specs=[vmem, vmem, whole...  7.46 us
  transfers between devices with their start and end apart: 13, of which 7 were waited for; matrix products, arithmetic and copies ran while one was open for 0% of the time, Pallas kernels for 16%

profile of v1, /device:TPU:1, one launch (start us, length us, event | category | flops | bytes accessed | tf_op | source)
XLA Modules:
  0.0 196.2 jit_solution(8771447043994821994)
XLA Ops:
  0.7 2.3 %split.1 = (bf16[16,16,1024]{2,1,0:T(8,128)(2,1)}, bf16[16,16,1024]{2,1,0:T(8,128)(2,1)}) custom-call(s32[1]{0:T(128)} %bitcast.same_at.start_ref, s32[1]{0:T(128)S(6)} %sub.15.other_at.start_ref, bf16[32,16,1024]{2,1,0:T(8,128)(2,1)} %bitcast.18), custom_call_target="tpu_custom_call" | custom-call | bytes 4194304 | tf_op jit(solution)/shard_map/split/pallas_call | solution.py:299
  2.9 3.1 %mix_same.1 = (bf16[256,1024]{1,0:T(8,128)(2,1)}, bf16[16,32,1024]{2,1,0:T(8,128)(2,1)}) custom-call(s32[1]{0:T(128)} %bitcast.same_at.start_ref, bf16[32,16,256]{2,1,0:T(8,128)(2,1)} %bitcast.15, bf16[256,1024]{1,0:T(8,128)(2,1)} %bitcast.20, bf16[16,16]{1,0:T(8,128)(2,1)} %bitcast.23, bf16[16,1024]{1,0:T(8,128)(2,1)} %embed_ref.3, ...), custom_call_target="tpu_custom_call" | custom-call | flops 268435456 | bytes 1048576 | tf_op jit(solution)/shard_map/mix_same/pallas_call | solution.py:309
  6.0 7.6 %all-to-all-start = ((bf16[16,32,1024]{2,1,0:T(8,128)(2,1)}), bf16[16,32,1024]{2,1,0:T(8,128)(2,1)S(1)}, u32[]{:S(2)}, u32[]{:S(2)}) async-start(bf16[16,32,1024]{2,1,0:T(8,128)(2,1)} %get-tuple-element.26), calls=%async_computation | async-start | bytes 2097152 | tf_op jit(solution)/shard_map/all_to_all | solution.py:282
  13.6 2.7 %mix_other.1 = (bf16[256,1024]{1,0:T(8,128)(2,1)}, bf16[16,16,1024]{2,1,0:T(8,128)(2,1)}) custom-call(s32[1]{0:T(128)S(6)} %sub.15.other_at.start_ref, bf16[32,16,256]{2,1,0:T(8,128)(2,1)} %bitcast.16, bf16[256,1024]{1,0:T(8,128)(2,1)} %bitcast.21, bf16[16,16]{1,0:T(8,128)(2,1)} %bitcast.24, bf16[16,1024]{1,0:T(8,128)(2,1)} %embed_ref.3), custom_call_target="tpu_custom_call" | custom-call | flops 268435456 | bytes 1048576 | tf_op jit(solution)/shard_map/mix_other/pallas_call | solution.py:290
  16.2 6.9 %collective-permute-start = (bf16[16,16,1024]{2,1,0:T(8,128)(2,1)}, bf16[16,16,1024]{2,1,0:T(8,128)(2,1)}, u32[]{:S(2)}, u32[]{:S(2)}) collective-permute-start(bf16[16,16,1024]{2,1,0:T(8,128)(2,1)} %get-tuple-element.27), channel_id=1, source_target_pairs={{0,32},{8,40},{16,48},{24,56},{32,0},{40,8},{48,16},{56,24},{64,96... | collective-permute-start | bytes 1572872 | tf_op jit(solution)/shard_map/ppermute | solution.py:286
  23.2 13.7 %collective-permute-done = bf16[16,16,1024]{2,1,0:T(8,128)(2,1)} collective-permute-done((bf16[16,16,1024]{2,1,0:T(8,128)(2,1)}, bf16[16,16,1024]{2,1,0:T(8,128)(2,1)}, u32[]{:S(2)}, u32[]{:S(2)}) %collective-permute-start) | collective-permute-done | bytes 524320 | tf_op jit(solution)/shard_map/ppermute | solution.py:286
  36.9 6.4 %all-to-all-start.1 = ((bf16[16,16,1024]{2,1,0:T(8,128)(2,1)}), bf16[16,16,1024]{2,1,0:T(8,128)(2,1)S(1)}, u32[]{:S(2)}, u32[]{:S(2)}) async-start(bf16[16,16,1024]{2,1,0:T(8,128)(2,1)} %collective-permute-done), calls=%async_computation.1 | async-start | bytes 1048576 | tf_op jit(solution)/shard_map/all_to_all | solution.py:282
  43.3 8.7 %collective-permute-done.2 = bf16[16,16,1024]{2,1,0:T(8,128)(2,1)} collective-permute-done((bf16[16,16,1024]{2,1,0:T(8,128)(2,1)}, bf16[16,16,1024]{2,1,0:T(8,128)(2,1)}, u32[]{:S(2)}, u32[]{:S(2)}) %collective-permute-start.2) | collective-permute-done | bytes 524320 | tf_op jit(solution)/shard_map/ppermute | solution.py:286
  52.5 5.9 %all-to-all-start.3 = ((bf16[16,16,1024]{2,1,0:T(8,128)(2,1)}), bf16[16,16,1024]{2,1,0:T(8,128)(2,1)S(1)}, u32[]{:S(2)}, u32[]{:S(2)}) async-start(bf16[16,16,1024]{2,1,0:T(8,128)(2,1)} %collective-permute-done.2), calls=%async_computation.3 | async-start | bytes 1048576 | tf_op jit(solution)/shard_map/all_to_all | solution.py:282
  58.5 7.5 %attend_project.1 = (bf16[512,1024]{1,0:T(8,128)(2,1)}, bf16[512,1024]{1,0:T(8,128)(2,1)}, bf16[512,1024]{1,0:T(8,128)(2,1)}, f32[512,1]{1,0:T(8,128)}) custom-call(bf16[16,32,1024]{2,1,0:T(8,128)(2,1)S(1)} %all-to-all-done.near_ref, bf16[16,16,1024]{2,1,0:T(8,128)(2,1)S(1)} %all-to-all-done.1.far_ref, f32[1,1024]{1,0:T(1,128)} %bitcast.26, ...), custom_call_target="tpu_custom_call" | custom-call | flops 3221225472 | bytes 10485760 | tf_op jit(solution)/shard_map/attend_project/pallas_call | solution.py:333
  66.0 8.9 %attend_forward.1 = (bf16[256,1024]{1,0:T(8,128)(2,1)}, bf16[256,1024]{1,0:T(8,128)(2,1)}, f32[8,512,512]{2,1,0:T(8,128)}) custom-call(bf16[16,32,1024]{2,1,0:T(8,128)(2,1)S(1)} %all-to-all-done.near_ref, bf16[16,16,1024]{2,1,0:T(8,128)(2,1)S(1)} %all-to-all-done.1.far_ref, bf16[512,1024]{1,0:T(8,128)(2,1)} %get-tuple-element.28.q_ref, ...), custom_call_target="tpu_custom_call" | custom-call | flops 1073741824 | bytes 14680064 | tf_op jit(solution)/shard_map/attend_forward/pallas_call | solution.py:344
  74.9 15.0 %attend_backward.1 = bf16[32,16,1024]{2,1,0:T(8,128)(2,1)} custom-call(s32[1]{0:T(128)S(6)} %mul.10.near_at, s32[1]{0:T(128)S(6)} %mul.11.far_at, bf16[16,32,1024]{2,1,0:T(8,128)(2,1)S(1)} %all-to-all-done.near_ref, bf16[16,16,1024]{2,1,0:T(8,128)(2,1)S(1)} %all-to-all-done.3.up_far_ref, bf16[512,1024]{1,0:T(8,128)(2,1)} %get-tuple-element.28.q_ref, ...), custom_call_target="tpu_custom_call" | custom-call | flops 5368709120 | bytes 16777216 | tf_op jit(solution)/shard_map/attend_backward/pallas_call | solution.py:354
  89.9 11.9 %all-to-all-start.4 = ((bf16[32,16,1024]{2,1,0:T(8,128)(2,1)}), bf16[32,16,1024]{2,1,0:T(8,128)(2,1)S(1)}, u32[]{:S(2)}, u32[]{:S(2)}) async-start(bf16[32,16,1024]{2,1,0:T(8,128)(2,1)} %attend_backward.1), calls=%async_computation.4 | async-start | bytes 2097152 | tf_op jit(solution)/shard_map/all_to_all | solution.py:372
  101.8 5.2 %collective-permute-start.1 = (bf16[16,16,1024]{2,1,0:T(8,128)(2,1)S(1)}, bf16[16,16,1024]{2,1,0:T(8,128)(2,1)S(1)}, u32[]{:S(2)}, u32[]{:S(2)}) collective-permute-start(bf16[16,16,1024]{2,1,0:T(8,128)(2,1)S(1)} %bitcast.28), channel_id=1, source_target_pairs={{0,32},{8,40},{16,48},{24,56},{32,0},{40,8},{48,16},{56,24},{64,96... | collective-permute-start | bytes 1572872 | tf_op jit(solution)/shard_map/ppermute | solution.py:286
  107.1 12.2 %collective-permute-done.1.other_ref = bf16[16,16,1024]{2,1,0:T(8,128)(2,1)S(1)} collective-permute-done((bf16[16,16,1024]{2,1,0:T(8,128)(2,1)S(1)}, bf16[16,16,1024]{2,1,0:T(8,128)(2,1)S(1)}, u32[]{:S(2)}, u32[]{:S(2)}) %collective-permute-start.1) | collective-permute-done | bytes 524320 | tf_op jit(solution)/shard_map/ppermute | solution.py:286
  119.3 0.8 copy-done.2
  120.0 2.2 %pack.1 = bf16[16,32,1024]{2,1,0:T(8,128)(2,1)} custom-call(bf16[16,16,1024]{2,1,0:T(8,128)(2,1)} %bitcast.22, bf16[16,16,1024]{2,1,0:T(8,128)(2,1)} %copy-done.2), custom_call_target="tpu_custom_call" | custom-call | bytes 4194304 | tf_op jit(solution)/shard_map/pack/pallas_call | solution.py:373
  122.3 6.5 %all-to-all-start.2 = ((bf16[16,32,1024]{2,1,0:T(8,128)(2,1)}), bf16[16,32,1024]{2,1,0:T(8,128)(2,1)S(1)}, u32[]{:S(2)}, u32[]{:S(2)}) async-start(bf16[16,32,1024]{2,1,0:T(8,128)(2,1)} %pack.1), calls=%async_computation.2 | async-start | bytes 2097152 | tf_op jit(solution)/shard_map/all_to_all | solution.py:282
  128.8 3.3 %side.1 = (f32[16,1152]{1,0:T(8,128)}, bf16[256,256]{1,0:T(8,128)(2,1)}, bf16[256,256]{1,0:T(8,128)(2,1)}, bf16[512,1024]{1,0:T(8,128)(2,1)}) custom-call(s32[1]{0:T(128)} %bitcast.same_at.start_ref, s32[1]{0:T(128)S(6)} %sub.15.other_at.start_ref, bf16[16,16,1024]{2,1,0:T(8,128)(2,1)} %get-tuple-element.25.upstream_ref.up_same_ref, ...), custom_call_target="tpu_custom_call" | custom-call | flops 268435456 | bytes 4194304 | tf_op jit(solution)/shard_map/side/pallas_call | solution.py:318
  132.1 0.9 copy-done.1
  133.0 2.6 %sums.1 = (f32[8,1152]{1,0:T(8,128)}, f32[8,1152]{1,0:T(8,128)}) custom-call(s32[1]{0:T(128)} %bitcast.11.core_ref, s32[1]{0:T(128)S(6)} %mul.10.near_at, s32[1]{0:T(128)S(6)} %mul.11.far_at, f32[16,1152]{1,0:T(8,128)S(1)} %copy-done.1, bf16[32,16,1024]{2,1,0:T(8,128)(2,1)S(1)} %all-to-all-done.4.branch_ref, bf16[512,1024]{1,0:T(8,128)(2,1)} %get-tuple-element.41.tokens_ref), custom_call_target="tpu_custom_call" | custom-call | flops 134217728 | bytes 4194304 | tf_op jit(solution)/shard_map/sums/pallas_call | solution.py:384
  135.6 40.9 %collective-permute-start.3 = (f32[8,1152]{1,0:T(8,128)}, f32[8,1152]{1,0:T(8,128)S(1)}, u32[]{:S(2)}, u32[]{:S(2)}) collective-permute-start(f32[8,1152]{1,0:T(8,128)} %get-tuple-element.43), channel_id=1, source_target_pairs={{0,1},{1,0},{2,3},{3,2},{4,5},{5,4},{6,7},{7,6},{8,9},{9,8},{10,11... | collective-permute-start | bytes 110600 | tf_op jit(solution)/shard_map/ppermute | solution.py:395
  176.5 1.1 collective-permute-done.3
  177.5 0.8 add.24
  178.3 1.9 collective-permute-start.5
  180.2 6.4 %collective-permute-start.6 = (f32[8,1152]{1,0:T(8,128)S(1)}, f32[8,1152]{1,0:T(8,128)S(1)}, u32[]{:S(2)}, u32[]{:S(2)}) collective-permute-start(f32[8,1152]{1,0:T(8,128)S(1)} %add.24), channel_id=1, source_target_pairs={{0,6},{1,7},{2,4},{3,5},{4,2},{5,3},{6,0},{7,1},{8,14},{9,15},{10,... | collective-permute-start | bytes 110600 | tf_op jit(solution)/shard_map/ppermute | solution.py:395
  186.7 1.0 place.1
  187.7 0.8 collective-permute-done.6
  188.5 1.4 collective-permute-done.4
  189.9 1.7 collective-permute-start.7
  191.6 3.9 %weight.1 = f32[256,1024]{1,0:T(8,128)} custom-call(s32[1]{0:T(128)S(6)} %mul.10.near_at, s32[1]{0:T(128)S(6)} %mul.11.far_at, bf16[16,16]{1,0:T(8,128)(2,1)} %bitcast.25, bf16[16,16,1024]{2,1,0:T(8,128)(2,1)} %get-tuple-element.25.upstream_ref.up_same_ref, bf16[16,16,1024]{2,1,0:T(8,128)(2,1)} %get-tuple-element.33.up_other_ref, ...), custom_call_target="tpu_custom_call" | custom-call | flops 536870912 | bytes 4194304 | tf_op jit(solution)/shard_map/weight/pallas_call | solution.py:406
  195.6 0.6 final.1
  (16 shorter events, 0.5 us)
Async XLA Ops:
  6.0 30.9 %all-to-all-start = ((bf16[16,32,1024]{2,1,0:T(8,128)(2,1)}), bf16[16,32,1024]{2,1,0:T(8,128)(2,1)S(1)}, u32[]{:S(2)}, u32[]{:S(2)}) async-start(bf16[16,32,1024]{2,1,0:T(8,128)(2,1)} %get-tuple-element.26), calls=%async_computation | async-start | bytes 2097152 | tf_op jit(solution)/shard_map/all_to_all | solution.py:282
  16.2 20.7 %collective-permute-start = (bf16[16,16,1024]{2,1,0:T(8,128)(2,1)}, bf16[16,16,1024]{2,1,0:T(8,128)(2,1)}, u32[]{:S(2)}, u32[]{:S(2)}) collective-permute-start(bf16[16,16,1024]{2,1,0:T(8,128)(2,1)} %get-tuple-element.27), channel_id=1, source_target_pairs={{0,32},{8,40},{16,48},{24,56},{32,0},{40,8},{48,16},{56,24},{64,96... | collective-permute-start | bytes 1572872 | tf_op jit(solution)/shard_map/ppermute | solution.py:286
  23.1 28.9 %collective-permute-start.2 = (bf16[16,16,1024]{2,1,0:T(8,128)(2,1)}, bf16[16,16,1024]{2,1,0:T(8,128)(2,1)}, u32[]{:S(2)}, u32[]{:S(2)}) collective-permute-start(bf16[16,16,1024]{2,1,0:T(8,128)(2,1)} %get-tuple-element.33.up_other_ref), channel_id=1, source_target_pairs={{0,32},{8,40},{16,48},{24,56},{32,0},{40,8},{48,16},{56,24},{64,96... | collective-permute-start | bytes 1572872 | tf_op jit(solution)/shard_map/ppermute | solution.py:286
  36.9 15.6 %all-to-all-start.1 = ((bf16[16,16,1024]{2,1,0:T(8,128)(2,1)}), bf16[16,16,1024]{2,1,0:T(8,128)(2,1)S(1)}, u32[]{:S(2)}, u32[]{:S(2)}) async-start(bf16[16,16,1024]{2,1,0:T(8,128)(2,1)} %collective-permute-done), calls=%async_computation.1 | async-start | bytes 1048576 | tf_op jit(solution)/shard_map/all_to_all | solution.py:282
  52.5 22.4 %all-to-all-start.3 = ((bf16[16,16,1024]{2,1,0:T(8,128)(2,1)}), bf16[16,16,1024]{2,1,0:T(8,128)(2,1)S(1)}, u32[]{:S(2)}, u32[]{:S(2)}) async-start(bf16[16,16,1024]{2,1,0:T(8,128)(2,1)} %collective-permute-done.2), calls=%async_computation.3 | async-start | bytes 1048576 | tf_op jit(solution)/shard_map/all_to_all | solution.py:282
  74.9 26.9 %copy-start.3 = (bf16[256,1024]{1,0:T(8,128)(2,1)S(1)}, bf16[256,1024]{1,0:T(8,128)(2,1)}, u32[]{:S(2)}) copy-start(bf16[256,1024]{1,0:T(8,128)(2,1)} %get-tuple-element.32) | copy-start | bytes 1572868
  89.9 32.4 %all-to-all-start.4 = ((bf16[32,16,1024]{2,1,0:T(8,128)(2,1)}), bf16[32,16,1024]{2,1,0:T(8,128)(2,1)S(1)}, u32[]{:S(2)}, u32[]{:S(2)}) async-start(bf16[32,16,1024]{2,1,0:T(8,128)(2,1)} %attend_backward.1), calls=%async_computation.4 | async-start | bytes 2097152 | tf_op jit(solution)/shard_map/all_to_all | solution.py:372
  101.8 17.4 %collective-permute-start.1 = (bf16[16,16,1024]{2,1,0:T(8,128)(2,1)S(1)}, bf16[16,16,1024]{2,1,0:T(8,128)(2,1)S(1)}, u32[]{:S(2)}, u32[]{:S(2)}) collective-permute-start(bf16[16,16,1024]{2,1,0:T(8,128)(2,1)S(1)} %bitcast.28), channel_id=1, source_target_pairs={{0,32},{8,40},{16,48},{24,56},{32,0},{40,8},{48,16},{56,24},{64,96... | collective-permute-start | bytes 1572872 | tf_op jit(solution)/shard_map/ppermute | solution.py:286
  119.2 0.8 copy-start.2
  122.3 69.3 %copy-start = (bf16[32,16,1024]{2,1,0:T(8,128)(2,1)}, bf16[32,16,1024]{2,1,0:T(8,128)(2,1)S(1)}, u32[]{:S(2)}) copy-start(bf16[32,16,1024]{2,1,0:T(8,128)(2,1)S(1)} %all-to-all-done.4.branch_ref) | copy-start | bytes 3145732
  122.3 64.4 %all-to-all-start.2 = ((bf16[16,32,1024]{2,1,0:T(8,128)(2,1)}), bf16[16,32,1024]{2,1,0:T(8,128)(2,1)S(1)}, u32[]{:S(2)}, u32[]{:S(2)}) async-start(bf16[16,32,1024]{2,1,0:T(8,128)(2,1)} %pack.1), calls=%async_computation.2 | async-start | bytes 2097152 | tf_op jit(solution)/shard_map/all_to_all | solution.py:282
  132.1 0.9 copy-start.1
  135.6 42.0 %collective-permute-start.3 = (f32[8,1152]{1,0:T(8,128)}, f32[8,1152]{1,0:T(8,128)S(1)}, u32[]{:S(2)}, u32[]{:S(2)}) collective-permute-start(f32[8,1152]{1,0:T(8,128)} %get-tuple-element.43), channel_id=1, source_target_pairs={{0,1},{1,0},{2,3},{3,2},{4,5},{5,4},{6,7},{7,6},{8,9},{9,8},{10,11... | collective-permute-start | bytes 110600 | tf_op jit(solution)/shard_map/ppermute | solution.py:395
  178.3 9.4 %collective-permute-start.5 = (f32[8,1152]{1,0:T(8,128)S(1)}, f32[8,1152]{1,0:T(8,128)S(1)}, u32[]{:S(2)}, u32[]{:S(2)}) collective-permute-start(f32[8,1152]{1,0:T(8,128)S(1)} %add.24), channel_id=1, source_target_pairs={{0,4},{1,5},{2,6},{3,7},{4,0},{5,1},{6,2},{7,3},{8,12},{9,13},{10,... | collective-permute-start | bytes 110600 | tf_op jit(solution)/shard_map/ppermute | solution.py:395
  180.2 8.3 %collective-permute-start.6 = (f32[8,1152]{1,0:T(8,128)S(1)}, f32[8,1152]{1,0:T(8,128)S(1)}, u32[]{:S(2)}, u32[]{:S(2)}) collective-permute-start(f32[8,1152]{1,0:T(8,128)S(1)} %add.24), channel_id=1, source_target_pairs={{0,6},{1,7},{2,4},{3,5},{4,2},{5,3},{6,0},{7,1},{8,14},{9,15},{10,... | collective-permute-start | bytes 110600 | tf_op jit(solution)/shard_map/ppermute | solution.py:395
  186.7 3.2 %collective-permute-start.4 = (f32[8,1152]{1,0:T(8,128)S(1)}, f32[8,1152]{1,0:T(8,128)S(1)}, u32[]{:S(2)}, u32[]{:S(2)}) collective-permute-start(f32[8,1152]{1,0:T(8,128)S(1)} %add.24), channel_id=1, source_target_pairs={{0,2},{1,3},{2,0},{3,1},{4,6},{5,7},{6,4},{7,5},{8,10},{9,11},{10,... | collective-permute-start | bytes 110600 | tf_op jit(solution)/shard_map/ppermute | solution.py:395
  189.9 5.7 %collective-permute-start.7 = (f32[8,1152]{1,0:T(8,128)S(1)}, f32[8,1152]{1,0:T(8,128)S(1)}, u32[]{:S(2)}, u32[]{:S(2)}) collective-permute-start(f32[8,1152]{1,0:T(8,128)S(1)} %add_add_fusion.mine_ref), channel_id=1, source_target_pairs={{0,1},{1,0},{2,3},{3,2},{4,5},{5,4},{6,7},{7,6},{8,9},{9,8},{10,11... | collective-permute-start | bytes 110600 | tf_op jit(solution)/shard_map/ppermute | solution.py:395

commit v2 on v1

--- a/solution.py
+++ b/solution.py
@@ -57,12 +57,15 @@
 
 
 def mix_near_kernel(
-    start_ref, patches_ref, weight_ref, mixing_ref, embed_ref, upstream_ref, tokens_ref, both_ref
-):
-    both_ref[:, :GROUP] = mix_block(
-        start_ref[0], patches_ref, weight_ref, mixing_ref, embed_ref, tokens_ref
-    )
-    both_ref[:, GROUP:] = upstream_ref[...]
+    near_at, far_at, patches_ref, weight_ref, mixing_ref, embed_ref, upstream_ref,
+    tokens_ref, sent_ref,
+):
+    for k, base in enumerate(BASE):
+        sent_ref[k, GROUP : 2 * GROUP] = upstream_ref[base + near_at[0]]
+        sent_ref[k, 2 * GROUP :] = upstream_ref[base + far_at[0]]
+    sent_ref[:, :GROUP] = mix_block(
+        near_at[0], patches_ref, weight_ref, mixing_ref, embed_ref, tokens_ref
+    )
 
 
 def pack_kernel(same_ref, other_ref, both_ref):
@@ -82,12 +85,14 @@
         out_ref[base + other_at[0]] = both_ref[k, GROUP:]
 
 
-def project_kernel(
-    near_ref, far_ref, gain_ref, wq_ref, wk_ref, wv_ref, q_ref, k_ref, v_ref, inv_ref, normed_ref
-):
-    half = normed_ref.shape[0] // 2
-
-    @pl.when(pl.program_id(0) == 0)
+def forward_kernel(
+    near_ref, far_ref, gain_ref, wq_ref, wk_ref, wv_ref,
+    first_ref, second_ref, q_ref, k_ref, v_ref, probs_ref, inv_ref, normed_ref,
+):
+    step = pl.program_id(0)
+    half = first_ref.shape[0]
+
+    @pl.when(step == 0)
     def _():
         for ref, at in ((near_ref, 0), (far_ref, half)):
             mixed = ref[:, :GROUP].reshape(half, -1).astype(F32)
@@ -99,18 +104,15 @@
     q_ref[...] = nn(normed, wq_ref[...]).astype(BF16)
     k_ref[...] = nn(normed, wk_ref[...]).astype(BF16)
     v_ref[...] = nn(normed, wv_ref[...]).astype(BF16)
-
-
-def forward_kernel(near_ref, far_ref, q_ref, k_ref, v_ref, first_ref, second_ref, probs_ref):
-    step = pl.program_id(0)
-    half = first_ref.shape[0]
-    for i in range(2):
-        cols = slice(i * HDIM, (i + 1) * HDIM)
-        scores = nt(k_ref[:, cols], q_ref[:, cols]) * (SCALE * math.log2(math.e))
-        exps = jnp.exp2(scores - jnp.max(scores, axis=0, keepdims=True))
+    spans = [slice(i * HDIM, (i + 1) * HDIM) for i in range(2)]
+    scores = [nt(k_ref[:, cols], q_ref[:, cols]) for cols in spans]
+    values = [v_ref[:, cols].T for cols in spans]
+    for i, cols in enumerate(spans):
+        peak = jnp.max(scores[i], axis=0, keepdims=True)
+        exps = jnp.exp2((scores[i] - peak) * (SCALE * math.log2(math.e)))
         probs = exps * (1.0 / jnp.sum(exps, axis=0, keepdims=True))
         probs_ref[i] = probs
-        attended = nn(v_ref[:, cols].T, probs.astype(BF16)).astype(BF16).T
+        attended = nn(values[i], probs.astype(BF16)).astype(BF16).T
         here = pl.ds(pl.multiple_of(step * PAIR, PAIR) + i * HDIM, HDIM)
         for ref, out_ref, at in ((near_ref, first_ref, 0), (far_ref, second_ref, half)):
             base = ref[:, :GROUP, here].reshape(half, HDIM).astype(F32)
@@ -129,7 +131,7 @@
         here = pl.ds(pl.multiple_of(step * PAIR, PAIR) + i * HDIM, HDIM)
         up = jnp.concatenate(
             [
-                near_ref[:, GROUP:, here].reshape(half, HDIM),
+                near_ref[:, GROUP : 2 * GROUP, here].reshape(half, HDIM),
                 up_far_ref[:, :, here].reshape(half, HDIM),
             ],
             axis=0,
@@ -296,6 +298,15 @@
         name="mix_other",
     )(far, patches, tok_weight, mixing, chan_embed)
     mixed_far = flip(mixed_far)
+    tok_same, sent = pl.pallas_call(
+        mix_near_kernel,
+        in_specs=[smem] * 2 + [vmem] * 5,
+        out_specs=[vmem] * 2,
+        out_shape=[shape((rows, width), BF16), shape((PLANE, 3 * GROUP, width), BF16)],
+        cost_estimate=cost(4 * rows * pix * width, 4 * rows * width),
+        name="mix_same",
+    )(near, far, patches, tok_weight, mixing, chan_embed, upstream)
+    near_post = spread(sent)
     up_same, up_other = pl.pallas_call(
         split_kernel,
         in_specs=[smem] * 2 + [vmem],
@@ -304,17 +315,6 @@
         cost_estimate=cost(0, 4 << 20),
         name="split",
     )(near, far, upstream)
-    up_far = flip(up_other)
-    double = shape((PLANE, 2 * GROUP, width), BF16)
-    tok_same, both = pl.pallas_call(
-        mix_near_kernel,
-        in_specs=[smem] + [vmem] * 5,
-        out_specs=[vmem] * 2,
-        out_shape=[shape((rows, width), BF16), double],
-        cost_estimate=cost(4 * rows * pix * width, 4 * rows * width),
-        name="mix_same",
-    )(near, patches, tok_weight, mixing, chan_embed, up_same)
-    both = spread(both)
     part, pix_same, pix_other, tokens = pl.pallas_call(
         side_kernel,
         in_specs=[smem] * 2 + [vmem] * 5,
@@ -325,31 +325,24 @@
         cost_estimate=cost(4 * rows * rows * width, 4 << 20),
         name="side",
     )(near, far, up_same, up_other, tok_same, tok_other, patches)
+    up_far = flip(near_post[:, 2 * GROUP :])
     mixed_far = spread(mixed_far)
     column = lambda part: pl.BlockSpec((width, PAIR), lambda i: (0, part * steps + i))
     heads = pl.BlockSpec((chans, PAIR), lambda i: (0, i))
     half_heads = pl.BlockSpec((rows, PAIR), lambda i: (0, i))
     pairs = pl.BlockSpec((2, chans, chans), lambda i: (i, 0, 0))
-    q, k, v, inv = pl.pallas_call(
-        project_kernel,
+    enc_same, enc_other, q, k, v, probs, inv = pl.pallas_call(
+        forward_kernel,
         grid=(steps,),
         in_specs=[vmem, vmem, whole((1, width)), column(0), column(1), column(2)],
-        out_specs=[heads, heads, heads, whole((chans, 1))],
-        out_shape=[shape((chans, width), BF16)] * 3 + [shape((chans, 1), F32)],
+        out_specs=[half_heads, half_heads, heads, heads, heads, pairs, whole((chans, 1))],
+        out_shape=[shape((rows, width), BF16)] * 2
+        + [shape((chans, width), BF16)] * 3
+        + [shape((HEADS, chans, chans), F32), shape((chans, 1), F32)],
         scratch_shapes=[pltpu.VMEM((chans, width), BF16)],
-        cost_estimate=cost(6 * chans * width * width, 10 << 20),
-        name="attend_project",
-    )(to_vmem(both), to_vmem(mixed_far), gain, qkv_weight, qkv_weight, qkv_weight)
-    up_far = spread(up_far)
-    enc_same, enc_other, probs = pl.pallas_call(
-        forward_kernel,
-        grid=(steps,),
-        in_specs=[vmem, vmem, heads, heads, heads],
-        out_specs=[half_heads, half_heads, pairs],
-        out_shape=[shape((rows, width), BF16)] * 2 + [shape((HEADS, chans, chans), F32)],
-        cost_estimate=cost(4 * chans * chans * width, 14 << 20),
+        cost_estimate=cost(6 * chans * width * width + 4 * chans * chans * width, 16 << 20),
         name="attend_forward",
-    )(to_vmem(both), to_vmem(mixed_far), q, k, v)
+    )(to_vmem(near_post), to_vmem(mixed_far), gain, qkv_weight, qkv_weight, qkv_weight)
     enc_far = flip(enc_other)
     branch = pl.pallas_call(
         backward_kernel,
@@ -365,11 +358,12 @@
         cost_estimate=cost(6 * chans * width * width + 8 * chans * chans * width, 16 << 20),
         name="attend_backward",
     )(
-        near_rank, far_rank, to_vmem(both), to_vmem(up_far), q, k, v, probs,
+        near_rank, far_rank, to_vmem(near_post), to_vmem(up_far), q, k, v, probs,
         qkv_weight, qkv_weight, qkv_weight, to_vmem(mixed_far), inv, gain,
     )
     order = [c for half in plane for c in half]
     branch = lax.all_to_all(branch, "chan", 0, 0, axis_index_groups=[order], tiled=True)
+    double = shape((PLANE, 2 * GROUP, width), BF16)
     encoded = pl.pallas_call(
         pack_kernel,
         in_specs=[vmem] * 2,

time: 198 us -> 179 us (0.904)
  starting transfers between devices: 101 us -> 70.5 us
  waiting for transfers between devices: 38.4 us -> 55.3 us
  Pallas kernels: 53.1 us -> 49.3 us
    ppermute x5, starting transfers between devices: 51 us -> 27.4 us  [swap(): return lax.ppermute(x, 'pos', [(p, p ^ bit) for p in ranks])]
    ppermute x3, waiting for transfers between devices: 34.7 us -> 48.8 us  [flip(): return lax.ppermute(x.reshape(PLANE, GROUP, width), 'chan', pairs)]
    all_to_all x4 -> x3, starting transfers between devices: 26.4 us -> 17.6 us  [spread(): return lax.all_to_all(x, 'chan', 0, 0, axis_index_groups=plane, tiled=True)]
    ppermute x3, starting transfers between devices: 12.2 us -> 17.4 us  [flip(): return lax.ppermute(x.reshape(PLANE, GROUP, width), 'chan', pairs)]
    pallas_call x3 -> x2, Pallas kernels: 19.4 us -> 15.6 us  [the longest x1 12.2 us: step(): pl.pallas_call(forward_kernel, grid=(steps,), in_specs=[vmem, vmem, whole...]
    all_to_all x1, starting transfers between devices: 11.9 us -> 8.12 us  [step(): lax.all_to_all(branch, 'chan', 0, 0, axis_index_groups=[order], tiled=True)]
    all_to_all x4 -> x3, waiting for transfers between devices: 0.45 us -> 3.88 us  [spread(): return lax.all_to_all(x, 'chan', 0, 0, axis_index_groups=plane, tiled=True)]
  transfers between devices with their start and end apart: 13 -> 12, of which waited for: 7 -> 6; matrix products, arithmetic and copies ran while one was open for 0% -> 0% of each run, Pallas kernels for 16% -> 17%
where the time goes in v2:
time: 179 us; the launch traced here: 178 us
  starting transfers between devices  70.5 us (39%)
  waiting for transfers between devices  55.3 us (31%)
  Pallas kernels  49.3 us (28%)
    ppermute x3, waiting for transfers between devices, flip(): return lax.ppermute(x.reshape(PLANE, GROUP, width), 'chan', pairs)  48.8 us
    ppermute x5, starting transfers between devices, swap(): return lax.ppermute(x, 'pos', [(p, p ^ bit) for p in ranks])  27.4 us
    all_to_all x3, starting transfers between devices, spread(): return lax.all_to_all(x, 'chan', 0, 0, axis_index_groups=plane, tiled=True)  17.6 us
    ppermute x3, starting transfers between devices, flip(): return lax.ppermute(x.reshape(PLANE, GROUP, width), 'chan', pairs)  17.4 us
    pallas_call x1, Pallas kernels, step(): pl.pallas_call(backward_kernel, grid=(steps,), in_specs=[smem] * 2 + [vme...  15 us
    pallas_call x1, Pallas kernels, step(): pl.pallas_call(forward_kernel, grid=(steps,), in_specs=[vmem, vmem, whole...  12.2 us
    all_to_all x1, starting transfers between devices, step(): lax.all_to_all(branch, 'chan', 0, 0, axis_index_groups=[order], tiled=True)  8.12 us
    pallas_call x1, Pallas kernels, step(): pl.pallas_call(weight_kernel, in_specs=[smem] * 2 + [vmem] * 6, out_specs...  3.92 us
  transfers between devices with their start and end apart: 12, of which 6 were waited for; matrix products, arithmetic and copies ran while one was open for 0% of the time, Pallas kernels for 17%

profile of v2, /device:TPU:1, one launch (start us, length us, event | category | flops | bytes accessed | tf_op | source)
XLA Modules:
  0.0 178.3 jit_solution(15453452389823438146)
XLA Ops:
  0.7 3.5 %mix_same.1 = (bf16[256,1024]{1,0:T(8,128)(2,1)}, bf16[16,48,1024]{2,1,0:T(8,128)(2,1)}) custom-call(s32[1]{0:T(128)} %bitcast.near_at.same_at, s32[1]{0:T(128)S(6)} %sub.15.far_at.start_ref.other_at, bf16[32,16,256]{2,1,0:T(8,128)(2,1)} %bitcast.17, bf16[256,1024]{1,0:T(8,128)(2,1)} %bitcast.21, bf16[16,16]{1,0:T(8,128)(2,1)} %bitcast.24, ...), custom_call_target="tpu_custom_call" | custom-call | flops 268435456 | bytes 1048576 | tf_op jit(solution)/shard_map/mix_same/pallas_call | solution.py:301
  4.1 7.6 %all-to-all-start = ((bf16[16,48,1024]{2,1,0:T(8,128)(2,1)}), bf16[16,48,1024]{2,1,0:T(8,128)(2,1)S(1)}, u32[]{:S(2)}, u32[]{:S(2)}) async-start(bf16[16,48,1024]{2,1,0:T(8,128)(2,1)} %get-tuple-element.25), calls=%async_computation | async-start | bytes 3145728 | tf_op jit(solution)/shard_map/all_to_all | solution.py:284
  11.7 2.7 %mix_other.1 = (bf16[256,1024]{1,0:T(8,128)(2,1)}, bf16[16,16,1024]{2,1,0:T(8,128)(2,1)}) custom-call(s32[1]{0:T(128)S(6)} %sub.15.far_at.start_ref.other_at, bf16[32,16,256]{2,1,0:T(8,128)(2,1)} %bitcast.18, bf16[256,1024]{1,0:T(8,128)(2,1)} %bitcast.22, bf16[16,16]{1,0:T(8,128)(2,1)} %bitcast.25, bf16[16,1024]{1,0:T(8,128)(2,1)} %embed_ref.3), custom_call_target="tpu_custom_call" | custom-call | flops 268435456 | bytes 1048576 | tf_op jit(solution)/shard_map/mix_other/pallas_call | solution.py:292
  14.4 6.9 %collective-permute-start = (bf16[16,16,1024]{2,1,0:T(8,128)(2,1)}, bf16[16,16,1024]{2,1,0:T(8,128)(2,1)}, u32[]{:S(2)}, u32[]{:S(2)}) collective-permute-start(bf16[16,16,1024]{2,1,0:T(8,128)(2,1)} %get-tuple-element.26), channel_id=1, source_target_pairs={{0,32},{8,40},{16,48},{24,56},{32,0},{40,8},{48,16},{56,24},{64,96... | collective-permute-start | bytes 1572872 | tf_op jit(solution)/shard_map/ppermute | solution.py:288
  21.3 13.8 %collective-permute-done = bf16[16,16,1024]{2,1,0:T(8,128)(2,1)} collective-permute-done((bf16[16,16,1024]{2,1,0:T(8,128)(2,1)}, bf16[16,16,1024]{2,1,0:T(8,128)(2,1)}, u32[]{:S(2)}, u32[]{:S(2)}) %collective-permute-start) | collective-permute-done | bytes 524320 | tf_op jit(solution)/shard_map/ppermute | solution.py:288
  35.1 0.0 all-to-all-done.near_ref
  35.1 6.4 %all-to-all-start.1 = ((bf16[16,16,1024]{2,1,0:T(8,128)(2,1)}), bf16[16,16,1024]{2,1,0:T(8,128)(2,1)S(1)}, u32[]{:S(2)}, u32[]{:S(2)}) async-start(bf16[16,16,1024]{2,1,0:T(8,128)(2,1)} %collective-permute-done), calls=%async_computation.1 | async-start | bytes 1048576 | tf_op jit(solution)/shard_map/all_to_all | solution.py:284
  41.5 5.3 %collective-permute-start.2 = (bf16[16,16,1024]{2,1,0:T(8,128)(2,1)S(1)}, bf16[16,16,1024]{2,1,0:T(8,128)(2,1)S(1)}, u32[]{:S(2)}, u32[]{:S(2)}) collective-permute-start(bf16[16,16,1024]{2,1,0:T(8,128)(2,1)S(1)} %slice.4), channel_id=1, source_target_pairs={{0,32},{8,40},{16,48},{24,56},{32,0},{40,8},{48,16},{56,24},{64,96... | collective-permute-start | bytes 1572872 | tf_op jit(solution)/shard_map/ppermute | solution.py:288
  46.8 3.9 %all-to-all-done.1.far_ref = bf16[16,16,1024]{2,1,0:T(8,128)(2,1)S(1)} async-done(((bf16[16,16,1024]{2,1,0:T(8,128)(2,1)}), bf16[16,16,1024]{2,1,0:T(8,128)(2,1)S(1)}, u32[]{:S(2)}, u32[]{:S(2)}) %all-to-all-start.1) | async-done | bytes 524320 | tf_op jit(solution)/shard_map/all_to_all | solution.py:284
  50.6 12.2 %attend_forward.1 = (bf16[256,1024]{1,0:T(8,128)(2,1)}, bf16[256,1024]{1,0:T(8,128)(2,1)}, bf16[512,1024]{1,0:T(8,128)(2,1)}, bf16[512,1024]{1,0:T(8,128)(2,1)},...) custom-call(bf16[16,48,1024]{2,1,0:T(8,128)(2,1)S(1)} %all-to-all-done.near_ref, ...), custom_call_target="tpu_custom_call" | custom-call | flops 4294967296 | bytes 16777216 | tf_op jit(solution)/shard_map/attend_forward/pallas_call | solution.py:334
  62.8 15.0 %attend_backward.1 = bf16[32,16,1024]{2,1,0:T(8,128)(2,1)} custom-call(s32[1]{0:T(128)S(6)} %mul.10.near_at, s32[1]{0:T(128)S(6)} %mul.11.far_at, bf16[16,48,1024]{2,1,0:T(8,128)(2,1)S(1)} %all-to-all-done.near_ref, bf16[16,16,1024]{2,1,0:T(8,128)(2,1)S(1)} %collective-permute-done.2.up_far_ref, bf16[512,1024]{1,0:T(8,128)(2,1)} %get-tuple-element.31.q_ref, ...), custom_call_target="tpu_custom_call" | custom-call | flops 5368709120 | bytes 16777216 | tf_op jit(solution)/shard_map/attend_backward/pallas_call | solution.py:347
  77.8 8.1 %all-to-all-start.3 = ((bf16[32,16,1024]{2,1,0:T(8,128)(2,1)}), bf16[32,16,1024]{2,1,0:T(8,128)(2,1)S(1)}, u32[]{:S(2)}, u32[]{:S(2)}) async-start(bf16[32,16,1024]{2,1,0:T(8,128)(2,1)} %attend_backward.1), calls=%async_computation.3 | async-start | bytes 2097152 | tf_op jit(solution)/shard_map/all_to_all | solution.py:365
  86.0 5.2 %collective-permute-start.1 = (bf16[16,16,1024]{2,1,0:T(8,128)(2,1)S(1)}, bf16[16,16,1024]{2,1,0:T(8,128)(2,1)S(1)}, u32[]{:S(2)}, u32[]{:S(2)}) collective-permute-start(bf16[16,16,1024]{2,1,0:T(8,128)(2,1)S(1)} %bitcast.29), channel_id=1, source_target_pairs={{0,32},{8,40},{16,48},{24,56},{32,0},{40,8},{48,16},{56,24},{64,96... | collective-permute-start | bytes 1572872 | tf_op jit(solution)/shard_map/ppermute | solution.py:288
  91.2 35.0 %collective-permute-done.1.other_ref = bf16[16,16,1024]{2,1,0:T(8,128)(2,1)S(1)} collective-permute-done((bf16[16,16,1024]{2,1,0:T(8,128)(2,1)S(1)}, bf16[16,16,1024]{2,1,0:T(8,128)(2,1)S(1)}, u32[]{:S(2)}, u32[]{:S(2)}) %collective-permute-start.1) | collective-permute-done | bytes 524320 | tf_op jit(solution)/shard_map/ppermute | solution.py:288
  126.2 0.8 copy-done.2
  127.0 2.2 %pack.1 = bf16[16,32,1024]{2,1,0:T(8,128)(2,1)} custom-call(bf16[16,16,1024]{2,1,0:T(8,128)(2,1)} %bitcast.23, bf16[16,16,1024]{2,1,0:T(8,128)(2,1)} %copy-done.2), custom_call_target="tpu_custom_call" | custom-call | bytes 4194304 | tf_op jit(solution)/shard_map/pack/pallas_call | solution.py:367
  129.3 3.7 %all-to-all-start.2 = ((bf16[16,32,1024]{2,1,0:T(8,128)(2,1)}), bf16[16,32,1024]{2,1,0:T(8,128)(2,1)S(1)}, u32[]{:S(2)}, u32[]{:S(2)}) async-start(bf16[16,32,1024]{2,1,0:T(8,128)(2,1)} %pack.1), calls=%async_computation.2 | async-start | bytes 2097152 | tf_op jit(solution)/shard_map/all_to_all | solution.py:284
  132.9 2.3 %split.1 = (bf16[16,16,1024]{2,1,0:T(8,128)(2,1)}, bf16[16,16,1024]{2,1,0:T(8,128)(2,1)}) custom-call(s32[1]{0:T(128)} %bitcast.near_at.same_at, s32[1]{0:T(128)S(6)} %sub.15.far_at.start_ref.other_at, bf16[32,16,1024]{2,1,0:T(8,128)(2,1)} %bitcast.15), custom_call_target="tpu_custom_call" | custom-call | bytes 4194304 | tf_op jit(solution)/shard_map/split/pallas_call | solution.py:310
  135.2 3.3 %side.1 = (f32[16,1152]{1,0:T(8,128)}, bf16[256,256]{1,0:T(8,128)(2,1)}, bf16[256,256]{1,0:T(8,128)(2,1)}, bf16[512,1024]{1,0:T(8,128)(2,1)}) custom-call(s32[1]{0:T(128)} %bitcast.near_at.same_at, s32[1]{0:T(128)S(6)} %sub.15.far_at.start_ref.other_at, bf16[16,16,1024]{2,1,0:T(8,128)(2,1)} %get-tuple-element.29.up_same_ref, ...), custom_call_target="tpu_custom_call" | custom-call | flops 268435456 | bytes 4194304 | tf_op jit(solution)/shard_map/side/pallas_call | solution.py:318
  138.5 0.9 copy-done.1
  139.4 2.6 %sums.1 = (f32[8,1152]{1,0:T(8,128)}, f32[8,1152]{1,0:T(8,128)}) custom-call(s32[1]{0:T(128)} %bitcast.11.core_ref, s32[1]{0:T(128)S(6)} %mul.10.near_at, s32[1]{0:T(128)S(6)} %mul.11.far_at, f32[16,1152]{1,0:T(8,128)S(1)} %copy-done.1, bf16[32,16,1024]{2,1,0:T(8,128)(2,1)S(1)} %all-to-all-done.3.branch_ref, bf16[512,1024]{1,0:T(8,128)(2,1)} %get-tuple-element.41.tokens_ref), custom_call_target="tpu_custom_call" | custom-call | flops 134217728 | bytes 4194304 | tf_op jit(solution)/shard_map/sums/pallas_call | solution.py:378
  142.0 14.7 %collective-permute-start.3 = (f32[8,1152]{1,0:T(8,128)}, f32[8,1152]{1,0:T(8,128)S(1)}, u32[]{:S(2)}, u32[]{:S(2)}) collective-permute-start(f32[8,1152]{1,0:T(8,128)} %get-tuple-element.43), channel_id=1, source_target_pairs={{0,1},{1,0},{2,3},{3,2},{4,5},{5,4},{6,7},{7,6},{8,9},{9,8},{10,11... | collective-permute-start | bytes 110600 | tf_op jit(solution)/shard_map/ppermute | solution.py:389
  156.7 1.1 collective-permute-done.3
  157.8 0.8 add.24
  158.5 8.6 %collective-permute-start.4 = (f32[8,1152]{1,0:T(8,128)S(1)}, f32[8,1152]{1,0:T(8,128)S(1)}, u32[]{:S(2)}, u32[]{:S(2)}) collective-permute-start(f32[8,1152]{1,0:T(8,128)S(1)} %add.24), channel_id=1, source_target_pairs={{0,2},{1,3},{2,0},{3,1},{4,6},{5,7},{6,4},{7,5},{8,10},{9,11},{10,... | collective-permute-start | bytes 110600 | tf_op jit(solution)/shard_map/ppermute | solution.py:389
  167.1 2.2 %collective-permute-start.6 = (f32[8,1152]{1,0:T(8,128)S(1)}, f32[8,1152]{1,0:T(8,128)S(1)}, u32[]{:S(2)}, u32[]{:S(2)}) collective-permute-start(f32[8,1152]{1,0:T(8,128)S(1)} %add.24), channel_id=1, source_target_pairs={{0,6},{1,7},{2,4},{3,5},{4,2},{5,3},{6,0},{7,1},{8,14},{9,15},{10,... | collective-permute-start | bytes 110600 | tf_op jit(solution)/shard_map/ppermute | solution.py:389
  169.3 1.0 place.1
  170.3 0.7 collective-permute-done.5
  171.0 0.8 collective-permute-done.6
  171.8 1.9 %collective-permute-start.7 = (f32[8,1152]{1,0:T(8,128)S(1)}, f32[8,1152]{1,0:T(8,128)S(1)}, u32[]{:S(2)}, u32[]{:S(2)}) collective-permute-start(f32[8,1152]{1,0:T(8,128)S(1)} %add_add_fusion.mine_ref), channel_id=1, source_target_pairs={{0,1},{1,0},{2,3},{3,2},{4,5},{5,4},{6,7},{7,6},{8,9},{9,8},{10,11... | collective-permute-start | bytes 110600 | tf_op jit(solution)/shard_map/ppermute | solution.py:389
  173.8 3.9 %weight.1 = f32[256,1024]{1,0:T(8,128)} custom-call(s32[1]{0:T(128)S(6)} %mul.10.near_at, s32[1]{0:T(128)S(6)} %mul.11.far_at, bf16[16,16]{1,0:T(8,128)(2,1)} %bitcast.26, bf16[16,16,1024]{2,1,0:T(8,128)(2,1)} %get-tuple-element.29.up_same_ref, bf16[16,16,1024]{2,1,0:T(8,128)(2,1)} %get-tuple-element.30.up_other_ref, bf16[32,16,1024]{2,1,0:T(8,128)(2,1)} %copy-done, ...), custom_call_target="tpu_custom_call" | custom-call | flops 536870912 | bytes 4194304 | tf_op jit(solution)/shard_map/weight/pallas_call | solution.py:400
  177.7 0.6 final.1
  (14 shorter events, 0.1 us)
Async XLA Ops:
  4.1 30.9 %all-to-all-start = ((bf16[16,48,1024]{2,1,0:T(8,128)(2,1)}), bf16[16,48,1024]{2,1,0:T(8,128)(2,1)S(1)}, u32[]{:S(2)}, u32[]{:S(2)}) async-start(bf16[16,48,1024]{2,1,0:T(8,128)(2,1)} %get-tuple-element.25), calls=%async_computation | async-start | bytes 3145728 | tf_op jit(solution)/shard_map/all_to_all | solution.py:284
  14.4 20.7 %collective-permute-start = (bf16[16,16,1024]{2,1,0:T(8,128)(2,1)}, bf16[16,16,1024]{2,1,0:T(8,128)(2,1)}, u32[]{:S(2)}, u32[]{:S(2)}) collective-permute-start(bf16[16,16,1024]{2,1,0:T(8,128)(2,1)} %get-tuple-element.26), channel_id=1, source_target_pairs={{0,32},{8,40},{16,48},{24,56},{32,0},{40,8},{48,16},{56,24},{64,96... | collective-permute-start | bytes 1572872 | tf_op jit(solution)/shard_map/ppermute | solution.py:288
  35.1 15.6 %all-to-all-start.1 = ((bf16[16,16,1024]{2,1,0:T(8,128)(2,1)}), bf16[16,16,1024]{2,1,0:T(8,128)(2,1)S(1)}, u32[]{:S(2)}, u32[]{:S(2)}) async-start(bf16[16,16,1024]{2,1,0:T(8,128)(2,1)} %collective-permute-done), calls=%async_computation.1 | async-start | bytes 1048576 | tf_op jit(solution)/shard_map/all_to_all | solution.py:284
  41.5 21.3 %collective-permute-start.2 = (bf16[16,16,1024]{2,1,0:T(8,128)(2,1)S(1)}, bf16[16,16,1024]{2,1,0:T(8,128)(2,1)S(1)}, u32[]{:S(2)}, u32[]{:S(2)}) collective-permute-start(bf16[16,16,1024]{2,1,0:T(8,128)(2,1)S(1)} %slice.4), channel_id=1, source_target_pairs={{0,32},{8,40},{16,48},{24,56},{32,0},{40,8},{48,16},{56,24},{64,96... | collective-permute-start | bytes 1572872 | tf_op jit(solution)/shard_map/ppermute | solution.py:288
  62.8 23.1 %copy-start.3 = (bf16[256,1024]{1,0:T(8,128)(2,1)S(1)}, bf16[256,1024]{1,0:T(8,128)(2,1)}, u32[]{:S(2)}) copy-start(bf16[256,1024]{1,0:T(8,128)(2,1)} %get-tuple-element.28) | copy-start | bytes 1572868
  77.8 51.4 %all-to-all-start.3 = ((bf16[32,16,1024]{2,1,0:T(8,128)(2,1)}), bf16[32,16,1024]{2,1,0:T(8,128)(2,1)S(1)}, u32[]{:S(2)}, u32[]{:S(2)}) async-start(bf16[32,16,1024]{2,1,0:T(8,128)(2,1)} %attend_backward.1), calls=%async_computation.3 | async-start | bytes 2097152 | tf_op jit(solution)/shard_map/all_to_all | solution.py:365
  86.0 40.3 %collective-permute-start.1 = (bf16[16,16,1024]{2,1,0:T(8,128)(2,1)S(1)}, bf16[16,16,1024]{2,1,0:T(8,128)(2,1)S(1)}, u32[]{:S(2)}, u32[]{:S(2)}) collective-permute-start(bf16[16,16,1024]{2,1,0:T(8,128)(2,1)S(1)} %bitcast.29), channel_id=1, source_target_pairs={{0,32},{8,40},{16,48},{24,56},{32,0},{40,8},{48,16},{56,24},{64,96... | collective-permute-start | bytes 1572872 | tf_op jit(solution)/shard_map/ppermute | solution.py:288
  126.2 0.8 copy-start.2
  129.3 44.5 %copy-start = (bf16[32,16,1024]{2,1,0:T(8,128)(2,1)}, bf16[32,16,1024]{2,1,0:T(8,128)(2,1)S(1)}, u32[]{:S(2)}) copy-start(bf16[32,16,1024]{2,1,0:T(8,128)(2,1)S(1)} %all-to-all-done.3.branch_ref) | copy-start | bytes 3145732
  129.3 40.0 %all-to-all-start.2 = ((bf16[16,32,1024]{2,1,0:T(8,128)(2,1)}), bf16[16,32,1024]{2,1,0:T(8,128)(2,1)S(1)}, u32[]{:S(2)}, u32[]{:S(2)}) async-start(bf16[16,32,1024]{2,1,0:T(8,128)(2,1)} %pack.1), calls=%async_computation.2 | async-start | bytes 2097152 | tf_op jit(solution)/shard_map/all_to_all | solution.py:284
  138.5 0.9 copy-start.1
  142.0 15.8 %collective-permute-start.3 = (f32[8,1152]{1,0:T(8,128)}, f32[8,1152]{1,0:T(8,128)S(1)}, u32[]{:S(2)}, u32[]{:S(2)}) collective-permute-start(f32[8,1152]{1,0:T(8,128)} %get-tuple-element.43), channel_id=1, source_target_pairs={{0,1},{1,0},{2,3},{3,2},{4,5},{5,4},{6,7},{7,6},{8,9},{9,8},{10,11... | collective-permute-start | bytes 110600 | tf_op jit(solution)/shard_map/ppermute | solution.py:389
  158.5 11.8 %collective-permute-start.4 = (f32[8,1152]{1,0:T(8,128)S(1)}, f32[8,1152]{1,0:T(8,128)S(1)}, u32[]{:S(2)}, u32[]{:S(2)}) collective-permute-start(f32[8,1152]{1,0:T(8,128)S(1)} %add.24), channel_id=1, source_target_pairs={{0,2},{1,3},{2,0},{3,1},{4,6},{5,7},{6,4},{7,5},{8,10},{9,11},{10,... | collective-permute-start | bytes 110600 | tf_op jit(solution)/shard_map/ppermute | solution.py:389
  167.1 3.9 %collective-permute-start.5 = (f32[8,1152]{1,0:T(8,128)S(1)}, f32[8,1152]{1,0:T(8,128)S(1)}, u32[]{:S(2)}, u32[]{:S(2)}) collective-permute-start(f32[8,1152]{1,0:T(8,128)S(1)} %add.24), channel_id=1, source_target_pairs={{0,4},{1,5},{2,6},{3,7},{4,0},{5,1},{6,2},{7,3},{8,12},{9,13},{10,... | collective-permute-start | bytes 110600 | tf_op jit(solution)/shard_map/ppermute | solution.py:389
  167.1 4.7 %collective-permute-start.6 = (f32[8,1152]{1,0:T(8,128)S(1)}, f32[8,1152]{1,0:T(8,128)S(1)}, u32[]{:S(2)}, u32[]{:S(2)}) collective-permute-start(f32[8,1152]{1,0:T(8,128)S(1)} %add.24), channel_id=1, source_target_pairs={{0,6},{1,7},{2,4},{3,5},{4,2},{5,3},{6,0},{7,1},{8,14},{9,15},{10,... | collective-permute-start | bytes 110600 | tf_op jit(solution)/shard_map/ppermute | solution.py:389
  171.8 5.9 %collective-permute-start.7 = (f32[8,1152]{1,0:T(8,128)S(1)}, f32[8,1152]{1,0:T(8,128)S(1)}, u32[]{:S(2)}, u32[]{:S(2)}) collective-permute-start(f32[8,1152]{1,0:T(8,128)S(1)} %add_add_fusion.mine_ref), channel_id=1, source_target_pairs={{0,1},{1,0},{2,3},{3,2},{4,5},{5,4},{6,7},{7,6},{8,9},{9,8},{10,11... | collective-permute-start | bytes 110600 | tf_op jit(solution)/shard_map/ppermute | solution.py:389

commit v3 on v2

--- a/solution.py
+++ b/solution.py
@@ -17,6 +17,7 @@
 X, HALVES, Y = 4, 2, 4
 PLANE = X * Y
 BASE = [x * HALVES * Y + y for x in range(X) for y in range(Y)]
+LIMIT = pltpu.CompilerParams(vmem_limit_bytes=58 << 20)
 F32 = jnp.float32
 BF16 = jnp.bfloat16
 
@@ -61,8 +62,7 @@
     tokens_ref, sent_ref,
 ):
     for k, base in enumerate(BASE):
-        sent_ref[k, GROUP : 2 * GROUP] = upstream_ref[base + near_at[0]]
-        sent_ref[k, 2 * GROUP :] = upstream_ref[base + far_at[0]]
+        sent_ref[k, GROUP:] = upstream_ref[base + far_at[0]]
     sent_ref[:, :GROUP] = mix_block(
         near_at[0], patches_ref, weight_ref, mixing_ref, embed_ref, tokens_ref
     )
@@ -131,7 +131,7 @@
         here = pl.ds(pl.multiple_of(step * PAIR, PAIR) + i * HDIM, HDIM)
         up = jnp.concatenate(
             [
-                near_ref[:, GROUP : 2 * GROUP, here].reshape(half, HDIM),
+                far_ref[:, GROUP:, here].reshape(half, HDIM),
                 up_far_ref[:, :, here].reshape(half, HDIM),
             ],
             axis=0,
@@ -298,11 +298,12 @@
         name="mix_other",
     )(far, patches, tok_weight, mixing, chan_embed)
     mixed_far = flip(mixed_far)
+    double = shape((PLANE, 2 * GROUP, width), BF16)
     tok_same, sent = pl.pallas_call(
         mix_near_kernel,
         in_specs=[smem] * 2 + [vmem] * 5,
         out_specs=[vmem] * 2,
-        out_shape=[shape((rows, width), BF16), shape((PLANE, 3 * GROUP, width), BF16)],
+        out_shape=[shape((rows, width), BF16), double],
         cost_estimate=cost(4 * rows * pix * width, 4 * rows * width),
         name="mix_same",
     )(near, far, patches, tok_weight, mixing, chan_embed, upstream)
@@ -325,8 +326,19 @@
         cost_estimate=cost(4 * rows * rows * width, 4 << 20),
         name="side",
     )(near, far, up_same, up_other, tok_same, tok_other, patches)
-    up_far = flip(near_post[:, 2 * GROUP :])
-    mixed_far = spread(mixed_far)
+    up_far = flip(near_post[:, GROUP:])
+
+    def pack(first, second):
+        return pl.pallas_call(
+            pack_kernel,
+            in_specs=[vmem] * 2,
+            out_specs=vmem,
+            out_shape=double,
+            cost_estimate=cost(0, 4 << 20),
+            compiler_params=LIMIT,
+        )(first.reshape(piece.shape), second.reshape(piece.shape))
+
+    far_post = spread(pack(mixed_far, up_same))
     column = lambda part: pl.BlockSpec((width, PAIR), lambda i: (0, part * steps + i))
     heads = pl.BlockSpec((chans, PAIR), lambda i: (0, i))
     half_heads = pl.BlockSpec((rows, PAIR), lambda i: (0, i))
@@ -341,8 +353,9 @@
         + [shape((HEADS, chans, chans), F32), shape((chans, 1), F32)],
         scratch_shapes=[pltpu.VMEM((chans, width), BF16)],
         cost_estimate=cost(6 * chans * width * width + 4 * chans * chans * width, 16 << 20),
+        compiler_params=LIMIT,
         name="attend_forward",
-    )(to_vmem(near_post), to_vmem(mixed_far), gain, qkv_weight, qkv_weight, qkv_weight)
+    )(to_vmem(near_post), to_vmem(far_post), gain, qkv_weight, qkv_weight, qkv_weight)
     enc_far = flip(enc_other)
     branch = pl.pallas_call(
         backward_kernel,
@@ -356,22 +369,15 @@
         out_shape=shape((count, GROUP, width), BF16),
         scratch_shapes=[pltpu.VMEM((chans, PAIR), BF16)] * 3 + [pltpu.VMEM((chans, width), F32)],
         cost_estimate=cost(6 * chans * width * width + 8 * chans * chans * width, 16 << 20),
+        compiler_params=LIMIT,
         name="attend_backward",
     )(
         near_rank, far_rank, to_vmem(near_post), to_vmem(up_far), q, k, v, probs,
-        qkv_weight, qkv_weight, qkv_weight, to_vmem(mixed_far), inv, gain,
+        qkv_weight, qkv_weight, qkv_weight, to_vmem(far_post), inv, gain,
     )
     order = [c for half in plane for c in half]
     branch = lax.all_to_all(branch, "chan", 0, 0, axis_index_groups=[order], tiled=True)
-    double = shape((PLANE, 2 * GROUP, width), BF16)
-    encoded = pl.pallas_call(
-        pack_kernel,
-        in_specs=[vmem] * 2,
-        out_specs=vmem,
-        out_shape=double,
-        cost_estimate=cost(0, 4 << 20),
-        name="pack",
-    )(enc_same.reshape(piece.shape), enc_far)
+    encoded = pack(enc_same, enc_far)
     encoded = spread(encoded)
     core = (lax.axis_index("pos") % 2).astype(jnp.int32).reshape(1)
     half = shape((GROUP // 2, width + HDIM), F32)

time: 179 us -> 187 us (1.045)
  starting transfers between devices: 70.5 us -> 93.7 us
  waiting for transfers between devices: 55.3 us -> 36.2 us
  Pallas kernels: 49.3 us -> 51.3 us
    ppermute x3, waiting for transfers between devices: 48.8 us -> 23.6 us  [flip(): return lax.ppermute(x.reshape(PLANE, GROUP, width), 'chan', pairs)]
    ppermute x5, starting transfers between devices: 27.4 us -> 50.4 us  [swap(): return lax.ppermute(x, 'pos', [(p, p ^ bit) for p in ranks])]
    all_to_all x3, waiting for transfers between devices: 3.88 us -> 9.37 us  [spread(): return lax.all_to_all(x, 'chan', 0, 0, axis_index_groups=plane, tiled=True)]
    all_to_all x3, starting transfers between devices: 17.6 us -> 20.4 us  [spread(): return lax.all_to_all(x, 'chan', 0, 0, axis_index_groups=plane, tiled=True)]
    all_to_all x1, starting transfers between devices: 8.12 us -> 5.51 us  [step(): lax.all_to_all(branch, 'chan', 0, 0, axis_index_groups=[order], tiled=True)]
    pallas_call x1 -> x2, Pallas kernels: 2.24 us -> 4.47 us  [pack(): pl.pallas_call(pack_kernel, in_specs=[vmem] * 2, out_specs=vmem, out_shap...]
  transfers between devices with their start and end apart: 12 -> 12, of which waited for: 6 -> 6; matrix products, arithmetic and copies ran while one was open for 0% -> 0% of each run, Pallas kernels for 17% -> 18%
where the time goes in v3:
time: 187 us; the launch traced here: 185 us
  starting transfers between devices  93.7 us (50%)
  Pallas kernels  51.3 us (27%)
  waiting for transfers between devices  36.2 us (19%)
  local copies, waits for them, and re-layouts  2.54 us (1%)
    ppermute x5, starting transfers between devices, swap(): return lax.ppermute(x, 'pos', [(p, p ^ bit) for p in ranks])  50.4 us
    ppermute x3, waiting for transfers between devices, flip(): return lax.ppermute(x.reshape(PLANE, GROUP, width), 'chan', pairs)  23.6 us
    all_to_all x3, starting transfers between devices, spread(): return lax.all_to_all(x, 'chan', 0, 0, axis_index_groups=plane, tiled=True)  20.4 us
    ppermute x3, starting transfers between devices, flip(): return lax.ppermute(x.reshape(PLANE, GROUP, width), 'chan', pairs)  17.4 us
    pallas_call x1, Pallas kernels, step(): pl.pallas_call(backward_kernel, grid=(steps,), in_specs=[smem] * 2 + [vme...  15 us
    pallas_call x1, Pallas kernels, step(): pl.pallas_call(forward_kernel, grid=(steps,), in_specs=[vmem, vmem, whole...  12.2 us
    all_to_all x3, waiting for transfers between devices, spread(): return lax.all_to_all(x, 'chan', 0, 0, axis_index_groups=plane, tiled=True)  9.37 us
    all_to_all x1, starting transfers between devices, step(): lax.all_to_all(branch, 'chan', 0, 0, axis_index_groups=[order], tiled=True)  5.51 us
  transfers between devices with their start and end apart: 12, of which 6 were waited for; matrix products, arithmetic and copies ran while one was open for 0% of the time, Pallas kernels for 18%

profile of v3, /device:TPU:1, one launch (start us, length us, event | category | flops | bytes accessed | tf_op | source)
XLA Modules:
  0.0 185.4 jit_solution(1673590423784463827)
XLA Ops:
  0.7 3.3 %mix_same.1 = (bf16[256,1024]{1,0:T(8,128)(2,1)}, bf16[16,32,1024]{2,1,0:T(8,128)(2,1)}) custom-call(s32[1]{0:T(128)} %bitcast.near_at.same_at, s32[1]{0:T(128)S(6)} %sub.15.far_at.start_ref.other_at, bf16[32,16,256]{2,1,0:T(8,128)(2,1)} %bitcast.17, bf16[256,1024]{1,0:T(8,128)(2,1)} %bitcast.21, bf16[16,16]{1,0:T(8,128)(2,1)} %bitcast.24, ...), custom_call_target="tpu_custom_call" | custom-call | flops 268435456 | bytes 1048576 | tf_op jit(solution)/shard_map/mix_same/pallas_call | solution.py:302
  3.9 7.6 %all-to-all-start = ((bf16[16,32,1024]{2,1,0:T(8,128)(2,1)}), bf16[16,32,1024]{2,1,0:T(8,128)(2,1)S(1)}, u32[]{:S(2)}, u32[]{:S(2)}) async-start(bf16[16,32,1024]{2,1,0:T(8,128)(2,1)} %get-tuple-element.25), calls=%async_computation | async-start | bytes 2097152 | tf_op jit(solution)/shard_map/all_to_all | solution.py:284
  11.5 2.7 %mix_other.1 = (bf16[256,1024]{1,0:T(8,128)(2,1)}, bf16[16,16,1024]{2,1,0:T(8,128)(2,1)}) custom-call(s32[1]{0:T(128)S(6)} %sub.15.far_at.start_ref.other_at, bf16[32,16,256]{2,1,0:T(8,128)(2,1)} %bitcast.18, bf16[256,1024]{1,0:T(8,128)(2,1)} %bitcast.22, bf16[16,16]{1,0:T(8,128)(2,1)} %bitcast.25, bf16[16,1024]{1,0:T(8,128)(2,1)} %embed_ref.3), custom_call_target="tpu_custom_call" | custom-call | flops 268435456 | bytes 1048576 | tf_op jit(solution)/shard_map/mix_other/pallas_call | solution.py:292
  14.2 6.9 %collective-permute-start = (bf16[16,16,1024]{2,1,0:T(8,128)(2,1)}, bf16[16,16,1024]{2,1,0:T(8,128)(2,1)S(1)}, u32[]{:S(2)}, u32[]{:S(2)}) collective-permute-start(bf16[16,16,1024]{2,1,0:T(8,128)(2,1)} %get-tuple-element.26), channel_id=1, source_target_pairs={{0,32},{8,40},{16,48},{24,56},{32,0},{40,8},{48,16},{56,24},{64,96... | collective-permute-start | bytes 1572872 | tf_op jit(solution)/shard_map/ppermute | solution.py:288
  21.1 2.3 %split.1 = (bf16[16,16,1024]{2,1,0:T(8,128)(2,1)}, bf16[16,16,1024]{2,1,0:T(8,128)(2,1)}) custom-call(s32[1]{0:T(128)} %bitcast.near_at.same_at, s32[1]{0:T(128)S(6)} %sub.15.far_at.start_ref.other_at, bf16[32,16,1024]{2,1,0:T(8,128)(2,1)} %bitcast.15), custom_call_target="tpu_custom_call" | custom-call | bytes 4194304 | tf_op jit(solution)/shard_map/split/pallas_call | solution.py:311
  23.4 11.4 %collective-permute-done.same_ref = bf16[16,16,1024]{2,1,0:T(8,128)(2,1)S(1)} collective-permute-done((bf16[16,16,1024]{2,1,0:T(8,128)(2,1)}, bf16[16,16,1024]{2,1,0:T(8,128)(2,1)S(1)}, u32[]{:S(2)}, u32[]{:S(2)}) %collective-permute-start) | collective-permute-done | bytes 524320 | tf_op jit(solution)/shard_map/ppermute | solution.py:288
  34.8 0.8 copy-done.2
  35.6 2.2 %shard_map.102 = bf16[16,32,1024]{2,1,0:T(8,128)(2,1)} custom-call(bf16[16,16,1024]{2,1,0:T(8,128)(2,1)} %copy-done.2, bf16[16,16,1024]{2,1,0:T(8,128)(2,1)} %get-tuple-element.27.other_ref.up_same_ref), custom_call_target="tpu_custom_call" | custom-call | bytes 4194304 | tf_op jit(solution)/shard_map/pallas_call | solution.py:332
  37.8 6.4 %all-to-all-start.1 = ((bf16[16,32,1024]{2,1,0:T(8,128)(2,1)}), bf16[16,32,1024]{2,1,0:T(8,128)(2,1)S(1)}, u32[]{:S(2)}, u32[]{:S(2)}) async-start(bf16[16,32,1024]{2,1,0:T(8,128)(2,1)} %shard_map.102), calls=%async_computation.1 | async-start | bytes 2097152 | tf_op jit(solution)/shard_map/all_to_all | solution.py:284
  44.2 5.3 %collective-permute-start.2 = (bf16[16,16,1024]{2,1,0:T(8,128)(2,1)S(1)}, bf16[16,16,1024]{2,1,0:T(8,128)(2,1)S(1)}, u32[]{:S(2)}, u32[]{:S(2)}) collective-permute-start(bf16[16,16,1024]{2,1,0:T(8,128)(2,1)S(1)} %slice.4), channel_id=1, source_target_pairs={{0,32},{8,40},{16,48},{24,56},{32,0},{40,8},{48,16},{56,24},{64,96... | collective-permute-start | bytes 1572872 | tf_op jit(solution)/shard_map/ppermute | solution.py:288
  49.5 9.4 %all-to-all-done.1.far_ref = bf16[16,32,1024]{2,1,0:T(8,128)(2,1)S(1)} async-done(((bf16[16,32,1024]{2,1,0:T(8,128)(2,1)}), bf16[16,32,1024]{2,1,0:T(8,128)(2,1)S(1)}, u32[]{:S(2)}, u32[]{:S(2)}) %all-to-all-start.1) | async-done | bytes 1048608 | tf_op jit(solution)/shard_map/all_to_all | solution.py:284
  58.9 12.2 %attend_forward.1 = (bf16[256,1024]{1,0:T(8,128)(2,1)}, bf16[256,1024]{1,0:T(8,128)(2,1)}, bf16[512,1024]{1,0:T(8,128)(2,1)}, bf16[512,1024]{1,0:T(8,128)(2,1)},...) custom-call(bf16[16,32,1024]{2,1,0:T(8,128)(2,1)S(1)} %all-to-all-done.near_ref, ...), custom_call_target="tpu_custom_call" | custom-call | flops 4294967296 | bytes 16777216 | tf_op jit(solution)/shard_map/attend_forward/pallas_call | solution.py:346
  71.1 15.0 %attend_backward.1 = bf16[32,16,1024]{2,1,0:T(8,128)(2,1)} custom-call(s32[1]{0:T(128)S(6)} %mul.10.near_at, s32[1]{0:T(128)S(6)} %mul.11.far_at, bf16[16,32,1024]{2,1,0:T(8,128)(2,1)S(1)} %all-to-all-done.near_ref, bf16[16,16,1024]{2,1,0:T(8,128)(2,1)S(1)} %collective-permute-done.2.up_far_ref, bf16[512,1024]{1,0:T(8,128)(2,1)} %get-tuple-element.31.q_ref, ...), custom_call_target="tpu_custom_call" | custom-call | flops 5368709120 | bytes 16777216 | tf_op jit(solution)/shard_map/attend_backward/pallas_call | solution.py:360
  86.1 5.5 %all-to-all-start.3 = ((bf16[32,16,1024]{2,1,0:T(8,128)(2,1)}), bf16[32,16,1024]{2,1,0:T(8,128)(2,1)S(1)}, u32[]{:S(2)}, u32[]{:S(2)}) async-start(bf16[32,16,1024]{2,1,0:T(8,128)(2,1)} %attend_backward.1), calls=%async_computation.3 | async-start | bytes 2097152 | tf_op jit(solution)/shard_map/all_to_all | solution.py:379
  91.6 5.2 %collective-permute-start.1 = (bf16[16,16,1024]{2,1,0:T(8,128)(2,1)S(1)}, bf16[16,16,1024]{2,1,0:T(8,128)(2,1)S(1)}, u32[]{:S(2)}, u32[]{:S(2)}) collective-permute-start(bf16[16,16,1024]{2,1,0:T(8,128)(2,1)S(1)} %bitcast.29), channel_id=1, source_target_pairs={{0,32},{8,40},{16,48},{24,56},{32,0},{40,8},{48,16},{56,24},{64,96... | collective-permute-start | bytes 1572872 | tf_op jit(solution)/shard_map/ppermute | solution.py:288
  96.8 12.2 %collective-permute-done.1.other_ref = bf16[16,16,1024]{2,1,0:T(8,128)(2,1)S(1)} collective-permute-done((bf16[16,16,1024]{2,1,0:T(8,128)(2,1)S(1)}, bf16[16,16,1024]{2,1,0:T(8,128)(2,1)S(1)}, u32[]{:S(2)}, u32[]{:S(2)}) %collective-permute-start.1) | collective-permute-done | bytes 524320 | tf_op jit(solution)/shard_map/ppermute | solution.py:288
  109.0 0.8 copy-done.3
  109.8 2.2 %shard_map.103 = bf16[16,32,1024]{2,1,0:T(8,128)(2,1)} custom-call(bf16[16,16,1024]{2,1,0:T(8,128)(2,1)} %bitcast.23, bf16[16,16,1024]{2,1,0:T(8,128)(2,1)} %copy-done.3), custom_call_target="tpu_custom_call" | custom-call | bytes 4194304 | tf_op jit(solution)/shard_map/pallas_call | solution.py:332
  112.1 6.5 %all-to-all-start.2 = ((bf16[16,32,1024]{2,1,0:T(8,128)(2,1)}), bf16[16,32,1024]{2,1,0:T(8,128)(2,1)S(1)}, u32[]{:S(2)}, u32[]{:S(2)}) async-start(bf16[16,32,1024]{2,1,0:T(8,128)(2,1)} %shard_map.103), calls=%async_computation.2 | async-start | bytes 2097152 | tf_op jit(solution)/shard_map/all_to_all | solution.py:284
  118.6 3.3 %side.1 = (f32[16,1152]{1,0:T(8,128)}, bf16[256,256]{1,0:T(8,128)(2,1)}, bf16[256,256]{1,0:T(8,128)(2,1)}, bf16[512,1024]{1,0:T(8,128)(2,1)}) custom-call(s32[1]{0:T(128)} %bitcast.near_at.same_at, s32[1]{0:T(128)S(6)} %sub.15.far_at.start_ref.other_at, bf16[16,16,1024]{2,1,0:T(8,128)(2,1)} %get-tuple-element.27.other_ref.up_same_ref, ...), custom_call_target="tpu_custom_call" | custom-call | flops 268435456 | bytes 4194304 | tf_op jit(solution)/shard_map/side/pallas_call | solution.py:319
  121.9 0.9 copy-done.1
  122.8 2.6 %sums.1 = (f32[8,1152]{1,0:T(8,128)}, f32[8,1152]{1,0:T(8,128)}) custom-call(s32[1]{0:T(128)} %bitcast.11.core_ref, s32[1]{0:T(128)S(6)} %mul.10.near_at, s32[1]{0:T(128)S(6)} %mul.11.far_at, f32[16,1152]{1,0:T(8,128)S(1)} %copy-done.1, bf16[32,16,1024]{2,1,0:T(8,128)(2,1)S(1)} %all-to-all-done.3.branch_ref, bf16[512,1024]{1,0:T(8,128)(2,1)} %get-tuple-element.41.tokens_ref), custom_call_target="tpu_custom_call" | custom-call | flops 134217728 | bytes 4194304 | tf_op jit(solution)/shard_map/sums/pallas_call | solution.py:384
  125.4 33.7 %collective-permute-start.3 = (f32[8,1152]{1,0:T(8,128)}, f32[8,1152]{1,0:T(8,128)S(1)}, u32[]{:S(2)}, u32[]{:S(2)}) collective-permute-start(f32[8,1152]{1,0:T(8,128)} %get-tuple-element.43), channel_id=1, source_target_pairs={{0,1},{1,0},{2,3},{3,2},{4,5},{5,4},{6,7},{7,6},{8,9},{9,8},{10,11... | collective-permute-start | bytes 110600 | tf_op jit(solution)/shard_map/ppermute | solution.py:395
  159.0 1.1 collective-permute-done.3
  160.1 0.8 add.24
  160.9 4.9 %collective-permute-start.5 = (f32[8,1152]{1,0:T(8,128)S(1)}, f32[8,1152]{1,0:T(8,128)S(1)}, u32[]{:S(2)}, u32[]{:S(2)}) collective-permute-start(f32[8,1152]{1,0:T(8,128)S(1)} %add.24), channel_id=1, source_target_pairs={{0,4},{1,5},{2,6},{3,7},{4,0},{5,1},{6,2},{7,3},{8,12},{9,13},{10,... | collective-permute-start | bytes 110600 | tf_op jit(solution)/shard_map/ppermute | solution.py:395
  165.8 10.1 %collective-permute-start.6 = (f32[8,1152]{1,0:T(8,128)S(1)}, f32[8,1152]{1,0:T(8,128)S(1)}, u32[]{:S(2)}, u32[]{:S(2)}) collective-permute-start(f32[8,1152]{1,0:T(8,128)S(1)} %add.24), channel_id=1, source_target_pairs={{0,6},{1,7},{2,4},{3,5},{4,2},{5,3},{6,0},{7,1},{8,14},{9,15},{10,... | collective-permute-start | bytes 110600 | tf_op jit(solution)/shard_map/ppermute | solution.py:395
  175.8 1.0 place.1
  176.9 0.8 collective-permute-done.6
  177.7 1.4 collective-permute-done.4
  179.1 1.7 collective-permute-start.7
  180.8 3.9 %weight.1 = f32[256,1024]{1,0:T(8,128)} custom-call(s32[1]{0:T(128)S(6)} %mul.10.near_at, s32[1]{0:T(128)S(6)} %mul.11.far_at, bf16[16,16]{1,0:T(8,128)(2,1)} %bitcast.26, bf16[16,16,1024]{2,1,0:T(8,128)(2,1)} %get-tuple-element.27.other_ref.up_same_ref, bf16[16,16,1024]{2,1,0:T(8,128)(2,1)} %get-tuple-element.30.up_other_ref, ...), custom_call_target="tpu_custom_call" | custom-call | flops 536870912 | bytes 4194304 | tf_op jit(solution)/shard_map/weight/pallas_call | solution.py:406
  (17 shorter events, 0.7 us)
Async XLA Ops:
  3.9 33.9 %all-to-all-start = ((bf16[16,32,1024]{2,1,0:T(8,128)(2,1)}), bf16[16,32,1024]{2,1,0:T(8,128)(2,1)S(1)}, u32[]{:S(2)}, u32[]{:S(2)}) async-start(bf16[16,32,1024]{2,1,0:T(8,128)(2,1)} %get-tuple-element.25), calls=%async_computation | async-start | bytes 2097152 | tf_op jit(solution)/shard_map/all_to_all | solution.py:284
  14.2 20.6 %collective-permute-start = (bf16[16,16,1024]{2,1,0:T(8,128)(2,1)}, bf16[16,16,1024]{2,1,0:T(8,128)(2,1)S(1)}, u32[]{:S(2)}, u32[]{:S(2)}) collective-permute-start(bf16[16,16,1024]{2,1,0:T(8,128)(2,1)} %get-tuple-element.26), channel_id=1, source_target_pairs={{0,32},{8,40},{16,48},{24,56},{32,0},{40,8},{48,16},{56,24},{64,96... | collective-permute-start | bytes 1572872 | tf_op jit(solution)/shard_map/ppermute | solution.py:288
  34.7 0.8 copy-start.2
  37.8 21.0 %all-to-all-start.1 = ((bf16[16,32,1024]{2,1,0:T(8,128)(2,1)}), bf16[16,32,1024]{2,1,0:T(8,128)(2,1)S(1)}, u32[]{:S(2)}, u32[]{:S(2)}) async-start(bf16[16,32,1024]{2,1,0:T(8,128)(2,1)} %shard_map.102), calls=%async_computation.1 | async-start | bytes 2097152 | tf_op jit(solution)/shard_map/all_to_all | solution.py:284
  44.2 26.8 %collective-permute-start.2 = (bf16[16,16,1024]{2,1,0:T(8,128)(2,1)S(1)}, bf16[16,16,1024]{2,1,0:T(8,128)(2,1)S(1)}, u32[]{:S(2)}, u32[]{:S(2)}) collective-permute-start(bf16[16,16,1024]{2,1,0:T(8,128)(2,1)S(1)} %slice.4), channel_id=1, source_target_pairs={{0,32},{8,40},{16,48},{24,56},{32,0},{40,8},{48,16},{56,24},{64,96... | collective-permute-start | bytes 1572872 | tf_op jit(solution)/shard_map/ppermute | solution.py:288
  71.1 20.5 %copy-start.4 = (bf16[256,1024]{1,0:T(8,128)(2,1)S(1)}, bf16[256,1024]{1,0:T(8,128)(2,1)}, u32[]{:S(2)}) copy-start(bf16[256,1024]{1,0:T(8,128)(2,1)} %get-tuple-element.29) | copy-start | bytes 1572868
  86.1 26.0 %all-to-all-start.3 = ((bf16[32,16,1024]{2,1,0:T(8,128)(2,1)}), bf16[32,16,1024]{2,1,0:T(8,128)(2,1)S(1)}, u32[]{:S(2)}, u32[]{:S(2)}) async-start(bf16[32,16,1024]{2,1,0:T(8,128)(2,1)} %attend_backward.1), calls=%async_computation.3 | async-start | bytes 2097152 | tf_op jit(solution)/shard_map/all_to_all | solution.py:379
  91.6 17.4 %collective-permute-start.1 = (bf16[16,16,1024]{2,1,0:T(8,128)(2,1)S(1)}, bf16[16,16,1024]{2,1,0:T(8,128)(2,1)S(1)}, u32[]{:S(2)}, u32[]{:S(2)}) collective-permute-start(bf16[16,16,1024]{2,1,0:T(8,128)(2,1)S(1)} %bitcast.29), channel_id=1, source_target_pairs={{0,32},{8,40},{16,48},{24,56},{32,0},{40,8},{48,16},{56,24},{64,96... | collective-permute-start | bytes 1572872 | tf_op jit(solution)/shard_map/ppermute | solution.py:288
  109.0 0.8 copy-start.3
  112.1 68.8 %copy-start = (bf16[32,16,1024]{2,1,0:T(8,128)(2,1)}, bf16[32,16,1024]{2,1,0:T(8,128)(2,1)S(1)}, u32[]{:S(2)}) copy-start(bf16[32,16,1024]{2,1,0:T(8,128)(2,1)S(1)} %all-to-all-done.3.branch_ref) | copy-start | bytes 3145732
  112.1 63.8 %all-to-all-start.2 = ((bf16[16,32,1024]{2,1,0:T(8,128)(2,1)}), bf16[16,32,1024]{2,1,0:T(8,128)(2,1)S(1)}, u32[]{:S(2)}, u32[]{:S(2)}) async-start(bf16[16,32,1024]{2,1,0:T(8,128)(2,1)} %shard_map.103), calls=%async_computation.2 | async-start | bytes 2097152 | tf_op jit(solution)/shard_map/all_to_all | solution.py:284
  121.9 0.9 copy-start.1
  125.4 34.7 %collective-permute-start.3 = (f32[8,1152]{1,0:T(8,128)}, f32[8,1152]{1,0:T(8,128)S(1)}, u32[]{:S(2)}, u32[]{:S(2)}) collective-permute-start(f32[8,1152]{1,0:T(8,128)} %get-tuple-element.43), channel_id=1, source_target_pairs={{0,1},{1,0},{2,3},{3,2},{4,5},{5,4},{6,7},{7,6},{8,9},{9,8},{10,11... | collective-permute-start | bytes 110600 | tf_op jit(solution)/shard_map/ppermute | solution.py:395
  160.9 16.0 %collective-permute-start.5 = (f32[8,1152]{1,0:T(8,128)S(1)}, f32[8,1152]{1,0:T(8,128)S(1)}, u32[]{:S(2)}, u32[]{:S(2)}) collective-permute-start(f32[8,1152]{1,0:T(8,128)S(1)} %add.24), channel_id=1, source_target_pairs={{0,4},{1,5},{2,6},{3,7},{4,0},{5,1},{6,2},{7,3},{8,12},{9,13},{10,... | collective-permute-start | bytes 110600 | tf_op jit(solution)/shard_map/ppermute | solution.py:395
  165.8 11.9 %collective-permute-start.6 = (f32[8,1152]{1,0:T(8,128)S(1)}, f32[8,1152]{1,0:T(8,128)S(1)}, u32[]{:S(2)}, u32[]{:S(2)}) collective-permute-start(f32[8,1152]{1,0:T(8,128)S(1)} %add.24), channel_id=1, source_target_pairs={{0,6},{1,7},{2,4},{3,5},{4,2},{5,3},{6,0},{7,1},{8,14},{9,15},{10,... | collective-permute-start | bytes 110600 | tf_op jit(solution)/shard_map/ppermute | solution.py:395
  175.8 3.2 %collective-permute-start.4 = (f32[8,1152]{1,0:T(8,128)S(1)}, f32[8,1152]{1,0:T(8,128)S(1)}, u32[]{:S(2)}, u32[]{:S(2)}) collective-permute-start(f32[8,1152]{1,0:T(8,128)S(1)} %add.24), channel_id=1, source_target_pairs={{0,2},{1,3},{2,0},{3,1},{4,6},{5,7},{6,4},{7,5},{8,10},{9,11},{10,... | collective-permute-start | bytes 110600 | tf_op jit(solution)/shard_map/ppermute | solution.py:395
  179.1 5.7 %collective-permute-start.7 = (f32[8,1152]{1,0:T(8,128)S(1)}, f32[8,1152]{1,0:T(8,128)S(1)}, u32[]{:S(2)}, u32[]{:S(2)}) collective-permute-start(f32[8,1152]{1,0:T(8,128)S(1)} %add_add_fusion.mine_ref), channel_id=1, source_target_pairs={{0,1},{1,0},{2,3},{3,2},{4,5},{5,4},{6,7},{7,6},{8,9},{9,8},{10,11... | collective-permute-start | bytes 110600 | tf_op jit(solution)/shard_map/ppermute | solution.py:395

commit v4 on v2

--- a/solution.py
+++ b/solution.py
@@ -17,6 +17,7 @@
 X, HALVES, Y = 4, 2, 4
 PLANE = X * Y
 BASE = [x * HALVES * Y + y for x in range(X) for y in range(Y)]
+LIMIT = pltpu.CompilerParams(vmem_limit_bytes=57 << 20)
 F32 = jnp.float32
 BF16 = jnp.bfloat16
 
@@ -356,6 +357,7 @@
         out_shape=shape((count, GROUP, width), BF16),
         scratch_shapes=[pltpu.VMEM((chans, PAIR), BF16)] * 3 + [pltpu.VMEM((chans, width), F32)],
         cost_estimate=cost(6 * chans * width * width + 8 * chans * chans * width, 16 << 20),
+        compiler_params=LIMIT,
         name="attend_backward",
     )(
         near_rank, far_rank, to_vmem(near_post), to_vmem(up_far), q, k, v, probs,
@@ -370,6 +372,7 @@
         out_specs=vmem,
         out_shape=double,
         cost_estimate=cost(0, 4 << 20),
+        compiler_params=LIMIT,
         name="pack",
     )(enc_same.reshape(piece.shape), enc_far)
     encoded = spread(encoded)
@@ -381,8 +384,9 @@
         out_specs=[vmem] * 2,
         out_shape=[half] * 2,
         cost_estimate=cost(2 * rows * rows * width, 4 << 20),
+        compiler_params=LIMIT,
         name="sums",
-    )(core, near_rank, far_rank, to_vmem(part), to_vmem(branch), tokens)
+    )(core, near_rank, far_rank, to_vmem(part), to_vmem(branch), to_vmem(tokens))
     ranks = range(lax.axis_size("pos"))
 
     def swap(x, bit):
@@ -404,7 +408,7 @@
         out_shape=shape((pix, width), F32),
         cost_estimate=cost(8 * rows * pix * width, 4 << 20),
         name="weight",
-    )(near_rank, far_rank, mixing, up_same, up_other, branch, pix_same, pix_other)
+    )(near_rank, far_rank, mixing, up_same, up_other, to_vmem(branch), pix_same, pix_other)
     encoded = pl.pallas_call(
         place_kernel,
         in_specs=[smem] * 2 + [vmem],

time: 179 us -> 179 us (level)
  transfers between devices with their start and end apart: 12 -> 12, of which waited for: 6 -> 6; matrix products, arithmetic and copies ran while one was open for 0% -> 0% of each run, Pallas kernels for 17% -> 16%
where the time goes in v4:
time: 179 us; the launch traced here: 178 us
  starting transfers between devices  70.5 us (39%)
  waiting for transfers between devices  55.3 us (31%)
  Pallas kernels  47.8 us (27%)
  local copies, waits for them, and re-layouts  2.95 us (2%)
    ppermute x3, waiting for transfers between devices, flip(): return lax.ppermute(x.reshape(PLANE, GROUP, width), 'chan', pairs)  48.8 us
    ppermute x5, starting transfers between devices, swap(): return lax.ppermute(x, 'pos', [(p, p ^ bit) for p in ranks])  27.4 us
    all_to_all x3, starting transfers between devices, spread(): return lax.all_to_all(x, 'chan', 0, 0, axis_index_groups=plane, tiled=True)  17.6 us
    ppermute x3, starting transfers between devices, flip(): return lax.ppermute(x.reshape(PLANE, GROUP, width), 'chan', pairs)  17.4 us
    pallas_call x1, Pallas kernels, step(): pl.pallas_call(backward_kernel, grid=(steps,), in_specs=[smem] * 2 + [vme...  15 us
    pallas_call x1, Pallas kernels, step(): pl.pallas_call(forward_kernel, grid=(steps,), in_specs=[vmem, vmem, whole...  12.2 us
    all_to_all x1, starting transfers between devices, step(): lax.all_to_all(branch, 'chan', 0, 0, axis_index_groups=[order], tiled=True)  8.12 us
    all_to_all x3, waiting for transfers between devices, spread(): return lax.all_to_all(x, 'chan', 0, 0, axis_index_groups=plane, tiled=True)  3.88 us
  transfers between devices with their start and end apart: 12, of which 6 were waited for; matrix products, arithmetic and copies ran while one was open for 0% of the time, Pallas kernels for 16%

profile of v4, /device:TPU:1, one launch (start us, length us, event | category | flops | bytes accessed | tf_op | source)
XLA Modules:
  0.0 178.1 jit_solution(2700287335981526738)
XLA Ops:
  0.7 3.5 %mix_same.1 = (bf16[256,1024]{1,0:T(8,128)(2,1)}, bf16[16,48,1024]{2,1,0:T(8,128)(2,1)}) custom-call(s32[1]{0:T(128)} %bitcast.near_at.same_at, s32[1]{0:T(128)S(6)} %sub.15.far_at.start_ref.other_at, bf16[32,16,256]{2,1,0:T(8,128)(2,1)} %bitcast.17, bf16[256,1024]{1,0:T(8,128)(2,1)} %bitcast.21, bf16[16,16]{1,0:T(8,128)(2,1)} %bitcast.24, ...), custom_call_target="tpu_custom_call" | custom-call | flops 268435456 | bytes 1048576 | tf_op jit(solution)/shard_map/mix_same/pallas_call | solution.py:302
  4.1 7.6 %all-to-all-start = ((bf16[16,48,1024]{2,1,0:T(8,128)(2,1)}), bf16[16,48,1024]{2,1,0:T(8,128)(2,1)S(1)}, u32[]{:S(2)}, u32[]{:S(2)}) async-start(bf16[16,48,1024]{2,1,0:T(8,128)(2,1)} %get-tuple-element.25), calls=%async_computation | async-start | bytes 3145728 | tf_op jit(solution)/shard_map/all_to_all | solution.py:285
  11.7 2.7 %mix_other.1 = (bf16[256,1024]{1,0:T(8,128)(2,1)}, bf16[16,16,1024]{2,1,0:T(8,128)(2,1)}) custom-call(s32[1]{0:T(128)S(6)} %sub.15.far_at.start_ref.other_at, bf16[32,16,256]{2,1,0:T(8,128)(2,1)} %bitcast.18, bf16[256,1024]{1,0:T(8,128)(2,1)} %bitcast.22, bf16[16,16]{1,0:T(8,128)(2,1)} %bitcast.25, bf16[16,1024]{1,0:T(8,128)(2,1)} %embed_ref.3), custom_call_target="tpu_custom_call" | custom-call | flops 268435456 | bytes 1048576 | tf_op jit(solution)/shard_map/mix_other/pallas_call | solution.py:293
  14.4 6.9 %collective-permute-start = (bf16[16,16,1024]{2,1,0:T(8,128)(2,1)}, bf16[16,16,1024]{2,1,0:T(8,128)(2,1)}, u32[]{:S(2)}, u32[]{:S(2)}) collective-permute-start(bf16[16,16,1024]{2,1,0:T(8,128)(2,1)} %get-tuple-element.26), channel_id=1, source_target_pairs={{0,32},{8,40},{16,48},{24,56},{32,0},{40,8},{48,16},{56,24},{64,96... | collective-permute-start | bytes 1572872 | tf_op jit(solution)/shard_map/ppermute | solution.py:289
  21.3 13.8 %collective-permute-done = bf16[16,16,1024]{2,1,0:T(8,128)(2,1)} collective-permute-done((bf16[16,16,1024]{2,1,0:T(8,128)(2,1)}, bf16[16,16,1024]{2,1,0:T(8,128)(2,1)}, u32[]{:S(2)}, u32[]{:S(2)}) %collective-permute-start) | collective-permute-done | bytes 524320 | tf_op jit(solution)/shard_map/ppermute | solution.py:289
  35.1 6.4 %all-to-all-start.1 = ((bf16[16,16,1024]{2,1,0:T(8,128)(2,1)}), bf16[16,16,1024]{2,1,0:T(8,128)(2,1)S(1)}, u32[]{:S(2)}, u32[]{:S(2)}) async-start(bf16[16,16,1024]{2,1,0:T(8,128)(2,1)} %collective-permute-done), calls=%async_computation.1 | async-start | bytes 1048576 | tf_op jit(solution)/shard_map/all_to_all | solution.py:285
  41.5 5.3 %collective-permute-start.2 = (bf16[16,16,1024]{2,1,0:T(8,128)(2,1)S(1)}, bf16[16,16,1024]{2,1,0:T(8,128)(2,1)S(1)}, u32[]{:S(2)}, u32[]{:S(2)}) collective-permute-start(bf16[16,16,1024]{2,1,0:T(8,128)(2,1)S(1)} %slice.4), channel_id=1, source_target_pairs={{0,32},{8,40},{16,48},{24,56},{32,0},{40,8},{48,16},{56,24},{64,96... | collective-permute-start | bytes 1572872 | tf_op jit(solution)/shard_map/ppermute | solution.py:289
  46.8 3.9 %all-to-all-done.1.far_ref = bf16[16,16,1024]{2,1,0:T(8,128)(2,1)S(1)} async-done(((bf16[16,16,1024]{2,1,0:T(8,128)(2,1)}), bf16[16,16,1024]{2,1,0:T(8,128)(2,1)S(1)}, u32[]{:S(2)}, u32[]{:S(2)}) %all-to-all-start.1) | async-done | bytes 524320 | tf_op jit(solution)/shard_map/all_to_all | solution.py:285
  50.6 12.2 %attend_forward.1 = (bf16[256,1024]{1,0:T(8,128)(2,1)}, bf16[256,1024]{1,0:T(8,128)(2,1)}, bf16[512,1024]{1,0:T(8,128)(2,1)}, bf16[512,1024]{1,0:T(8,128)(2,1)},...) custom-call(bf16[16,48,1024]{2,1,0:T(8,128)(2,1)S(1)} %all-to-all-done.near_ref, ...), custom_call_target="tpu_custom_call" | custom-call | flops 4294967296 | bytes 16777216 | tf_op jit(solution)/shard_map/attend_forward/pallas_call | solution.py:335
  62.8 15.0 %attend_backward.1 = bf16[32,16,1024]{2,1,0:T(8,128)(2,1)} custom-call(s32[1]{0:T(128)S(6)} %mul.10.near_at, s32[1]{0:T(128)S(6)} %mul.11.far_at, bf16[16,48,1024]{2,1,0:T(8,128)(2,1)S(1)} %all-to-all-done.near_ref, bf16[16,16,1024]{2,1,0:T(8,128)(2,1)S(1)} %collective-permute-done.2.up_far_ref, bf16[512,1024]{1,0:T(8,128)(2,1)} %get-tuple-element.31.q_ref, ...), custom_call_target="tpu_custom_call" | custom-call | flops 5368709120 | bytes 16777216 | tf_op jit(solution)/shard_map/attend_backward/pallas_call | solution.py:348
  77.8 8.1 %all-to-all-start.3 = ((bf16[32,16,1024]{2,1,0:T(8,128)(2,1)}), bf16[32,16,1024]{2,1,0:T(8,128)(2,1)S(1)}, u32[]{:S(2)}, u32[]{:S(2)}) async-start(bf16[32,16,1024]{2,1,0:T(8,128)(2,1)} %attend_backward.1), calls=%async_computation.3 | async-start | bytes 2097152 | tf_op jit(solution)/shard_map/all_to_all | solution.py:367
  86.0 5.2 %collective-permute-start.1 = (bf16[16,16,1024]{2,1,0:T(8,128)(2,1)S(1)}, bf16[16,16,1024]{2,1,0:T(8,128)(2,1)S(1)}, u32[]{:S(2)}, u32[]{:S(2)}) collective-permute-start(bf16[16,16,1024]{2,1,0:T(8,128)(2,1)S(1)} %bitcast.29), channel_id=1, source_target_pairs={{0,32},{8,40},{16,48},{24,56},{32,0},{40,8},{48,16},{56,24},{64,96... | collective-permute-start | bytes 1572872 | tf_op jit(solution)/shard_map/ppermute | solution.py:289
  91.2 35.0 %collective-permute-done.1.other_ref = bf16[16,16,1024]{2,1,0:T(8,128)(2,1)S(1)} collective-permute-done((bf16[16,16,1024]{2,1,0:T(8,128)(2,1)S(1)}, bf16[16,16,1024]{2,1,0:T(8,128)(2,1)S(1)}, u32[]{:S(2)}, u32[]{:S(2)}) %collective-permute-start.1) | collective-permute-done | bytes 524320 | tf_op jit(solution)/shard_map/ppermute | solution.py:289
  126.2 0.8 copy-done.2
  127.0 2.2 %pack.1 = bf16[16,32,1024]{2,1,0:T(8,128)(2,1)} custom-call(bf16[16,16,1024]{2,1,0:T(8,128)(2,1)} %bitcast.23, bf16[16,16,1024]{2,1,0:T(8,128)(2,1)} %copy-done.2), custom_call_target="tpu_custom_call" | custom-call | bytes 4194304 | tf_op jit(solution)/shard_map/pack/pallas_call | solution.py:369
  129.3 3.7 %all-to-all-start.2 = ((bf16[16,32,1024]{2,1,0:T(8,128)(2,1)}), bf16[16,32,1024]{2,1,0:T(8,128)(2,1)S(1)}, u32[]{:S(2)}, u32[]{:S(2)}) async-start(bf16[16,32,1024]{2,1,0:T(8,128)(2,1)} %pack.1), calls=%async_computation.2 | async-start | bytes 2097152 | tf_op jit(solution)/shard_map/all_to_all | solution.py:285
  132.9 2.3 %split.1 = (bf16[16,16,1024]{2,1,0:T(8,128)(2,1)}, bf16[16,16,1024]{2,1,0:T(8,128)(2,1)}) custom-call(s32[1]{0:T(128)} %bitcast.near_at.same_at, s32[1]{0:T(128)S(6)} %sub.15.far_at.start_ref.other_at, bf16[32,16,1024]{2,1,0:T(8,128)(2,1)} %bitcast.15), custom_call_target="tpu_custom_call" | custom-call | bytes 4194304 | tf_op jit(solution)/shard_map/split/pallas_call | solution.py:311
  135.2 3.3 %side.1 = (f32[16,1152]{1,0:T(8,128)}, bf16[256,256]{1,0:T(8,128)(2,1)}, bf16[256,256]{1,0:T(8,128)(2,1)}, bf16[512,1024]{1,0:T(8,128)(2,1)}) custom-call(s32[1]{0:T(128)} %bitcast.near_at.same_at, s32[1]{0:T(128)S(6)} %sub.15.far_at.start_ref.other_at, bf16[16,16,1024]{2,1,0:T(8,128)(2,1)} %get-tuple-element.29.up_same_ref, ...), custom_call_target="tpu_custom_call" | custom-call | flops 268435456 | bytes 4194304 | tf_op jit(solution)/shard_map/side/pallas_call | solution.py:319
  138.5 1.2 copy-done
  139.8 0.9 copy-done.1
  140.6 1.3 sums.1
  142.0 14.7 %collective-permute-start.3 = (f32[8,1152]{1,0:T(8,128)}, f32[8,1152]{1,0:T(8,128)S(1)}, u32[]{:S(2)}, u32[]{:S(2)}) collective-permute-start(f32[8,1152]{1,0:T(8,128)} %get-tuple-element.43), channel_id=1, source_target_pairs={{0,1},{1,0},{2,3},{3,2},{4,5},{5,4},{6,7},{7,6},{8,9},{9,8},{10,11... | collective-permute-start | bytes 110600 | tf_op jit(solution)/shard_map/ppermute | solution.py:393
  156.7 1.1 collective-permute-done.3
  157.8 0.8 add.24
  158.6 8.6 %collective-permute-start.4 = (f32[8,1152]{1,0:T(8,128)S(1)}, f32[8,1152]{1,0:T(8,128)S(1)}, u32[]{:S(2)}, u32[]{:S(2)}) collective-permute-start(f32[8,1152]{1,0:T(8,128)S(1)} %add.24), channel_id=1, source_target_pairs={{0,2},{1,3},{2,0},{3,1},{4,6},{5,7},{6,4},{7,5},{8,10},{9,11},{10,... | collective-permute-start | bytes 110600 | tf_op jit(solution)/shard_map/ppermute | solution.py:393
  167.2 2.2 %collective-permute-start.6 = (f32[8,1152]{1,0:T(8,128)S(1)}, f32[8,1152]{1,0:T(8,128)S(1)}, u32[]{:S(2)}, u32[]{:S(2)}) collective-permute-start(f32[8,1152]{1,0:T(8,128)S(1)} %add.24), channel_id=1, source_target_pairs={{0,6},{1,7},{2,4},{3,5},{4,2},{5,3},{6,0},{7,1},{8,14},{9,15},{10,... | collective-permute-start | bytes 110600 | tf_op jit(solution)/shard_map/ppermute | solution.py:393
  169.3 1.0 place.1
  170.4 0.7 collective-permute-done.5
  171.1 0.8 collective-permute-done.6
  171.9 1.9 %collective-permute-start.7 = (f32[8,1152]{1,0:T(8,128)S(1)}, f32[8,1152]{1,0:T(8,128)S(1)}, u32[]{:S(2)}, u32[]{:S(2)}) collective-permute-start(f32[8,1152]{1,0:T(8,128)S(1)} %add_add_fusion.mine_ref), channel_id=1, source_target_pairs={{0,1},{1,0},{2,3},{3,2},{4,5},{5,4},{6,7},{7,6},{8,9},{9,8},{10,11... | collective-permute-start | bytes 110600 | tf_op jit(solution)/shard_map/ppermute | solution.py:393
  173.8 3.6 %weight.1 = f32[256,1024]{1,0:T(8,128)} custom-call(s32[1]{0:T(128)S(6)} %mul.10.near_at, s32[1]{0:T(128)S(6)} %mul.11.far_at, bf16[16,16]{1,0:T(8,128)(2,1)} %bitcast.26, bf16[16,16,1024]{2,1,0:T(8,128)(2,1)} %get-tuple-element.29.up_same_ref, bf16[16,16,1024]{2,1,0:T(8,128)(2,1)} %get-tuple-element.30.up_other_ref, ...), custom_call_target="tpu_custom_call" | custom-call | flops 536870912 | bytes 4194304 | tf_op jit(solution)/shard_map/weight/pallas_call | solution.py:404
  177.4 0.6 final.1
  (14 shorter events, 0.1 us)
Async XLA Ops:
  4.1 30.9 %all-to-all-start = ((bf16[16,48,1024]{2,1,0:T(8,128)(2,1)}), bf16[16,48,1024]{2,1,0:T(8,128)(2,1)S(1)}, u32[]{:S(2)}, u32[]{:S(2)}) async-start(bf16[16,48,1024]{2,1,0:T(8,128)(2,1)} %get-tuple-element.25), calls=%async_computation | async-start | bytes 3145728 | tf_op jit(solution)/shard_map/all_to_all | solution.py:285
  14.4 20.7 %collective-permute-start = (bf16[16,16,1024]{2,1,0:T(8,128)(2,1)}, bf16[16,16,1024]{2,1,0:T(8,128)(2,1)}, u32[]{:S(2)}, u32[]{:S(2)}) collective-permute-start(bf16[16,16,1024]{2,1,0:T(8,128)(2,1)} %get-tuple-element.26), channel_id=1, source_target_pairs={{0,32},{8,40},{16,48},{24,56},{32,0},{40,8},{48,16},{56,24},{64,96... | collective-permute-start | bytes 1572872 | tf_op jit(solution)/shard_map/ppermute | solution.py:289
  35.1 15.6 %all-to-all-start.1 = ((bf16[16,16,1024]{2,1,0:T(8,128)(2,1)}), bf16[16,16,1024]{2,1,0:T(8,128)(2,1)S(1)}, u32[]{:S(2)}, u32[]{:S(2)}) async-start(bf16[16,16,1024]{2,1,0:T(8,128)(2,1)} %collective-permute-done), calls=%async_computation.1 | async-start | bytes 1048576 | tf_op jit(solution)/shard_map/all_to_all | solution.py:285
  41.5 21.3 %collective-permute-start.2 = (bf16[16,16,1024]{2,1,0:T(8,128)(2,1)S(1)}, bf16[16,16,1024]{2,1,0:T(8,128)(2,1)S(1)}, u32[]{:S(2)}, u32[]{:S(2)}) collective-permute-start(bf16[16,16,1024]{2,1,0:T(8,128)(2,1)S(1)} %slice.4), channel_id=1, source_target_pairs={{0,32},{8,40},{16,48},{24,56},{32,0},{40,8},{48,16},{56,24},{64,96... | collective-permute-start | bytes 1572872 | tf_op jit(solution)/shard_map/ppermute | solution.py:289
  62.8 23.1 %copy-start.3 = (bf16[256,1024]{1,0:T(8,128)(2,1)S(1)}, bf16[256,1024]{1,0:T(8,128)(2,1)}, u32[]{:S(2)}) copy-start(bf16[256,1024]{1,0:T(8,128)(2,1)} %get-tuple-element.28) | copy-start | bytes 1572868
  77.8 51.4 %all-to-all-start.3 = ((bf16[32,16,1024]{2,1,0:T(8,128)(2,1)}), bf16[32,16,1024]{2,1,0:T(8,128)(2,1)S(1)}, u32[]{:S(2)}, u32[]{:S(2)}) async-start(bf16[32,16,1024]{2,1,0:T(8,128)(2,1)} %attend_backward.1), calls=%async_computation.3 | async-start | bytes 2097152 | tf_op jit(solution)/shard_map/all_to_all | solution.py:367
  86.0 40.3 %collective-permute-start.1 = (bf16[16,16,1024]{2,1,0:T(8,128)(2,1)S(1)}, bf16[16,16,1024]{2,1,0:T(8,128)(2,1)S(1)}, u32[]{:S(2)}, u32[]{:S(2)}) collective-permute-start(bf16[16,16,1024]{2,1,0:T(8,128)(2,1)S(1)} %bitcast.29), channel_id=1, source_target_pairs={{0,32},{8,40},{16,48},{24,56},{32,0},{40,8},{48,16},{56,24},{64,96... | collective-permute-start | bytes 1572872 | tf_op jit(solution)/shard_map/ppermute | solution.py:289
  126.2 0.8 copy-start.2
  129.3 40.0 %all-to-all-start.2 = ((bf16[16,32,1024]{2,1,0:T(8,128)(2,1)}), bf16[16,32,1024]{2,1,0:T(8,128)(2,1)S(1)}, u32[]{:S(2)}, u32[]{:S(2)}) async-start(bf16[16,32,1024]{2,1,0:T(8,128)(2,1)} %pack.1), calls=%async_computation.2 | async-start | bytes 2097152 | tf_op jit(solution)/shard_map/all_to_all | solution.py:285
  138.5 1.2 copy-start
  139.8 0.9 copy-start.1
  142.0 15.8 %collective-permute-start.3 = (f32[8,1152]{1,0:T(8,128)}, f32[8,1152]{1,0:T(8,128)S(1)}, u32[]{:S(2)}, u32[]{:S(2)}) collective-permute-start(f32[8,1152]{1,0:T(8,128)} %get-tuple-element.43), channel_id=1, source_target_pairs={{0,1},{1,0},{2,3},{3,2},{4,5},{5,4},{6,7},{7,6},{8,9},{9,8},{10,11... | collective-permute-start | bytes 110600 | tf_op jit(solution)/shard_map/ppermute | solution.py:393
  158.6 11.8 %collective-permute-start.4 = (f32[8,1152]{1,0:T(8,128)S(1)}, f32[8,1152]{1,0:T(8,128)S(1)}, u32[]{:S(2)}, u32[]{:S(2)}) collective-permute-start(f32[8,1152]{1,0:T(8,128)S(1)} %add.24), channel_id=1, source_target_pairs={{0,2},{1,3},{2,0},{3,1},{4,6},{5,7},{6,4},{7,5},{8,10},{9,11},{10,... | collective-permute-start | bytes 110600 | tf_op jit(solution)/shard_map/ppermute | solution.py:393
  167.1 3.9 %collective-permute-start.5 = (f32[8,1152]{1,0:T(8,128)S(1)}, f32[8,1152]{1,0:T(8,128)S(1)}, u32[]{:S(2)}, u32[]{:S(2)}) collective-permute-start(f32[8,1152]{1,0:T(8,128)S(1)} %add.24), channel_id=1, source_target_pairs={{0,4},{1,5},{2,6},{3,7},{4,0},{5,1},{6,2},{7,3},{8,12},{9,13},{10,... | collective-permute-start | bytes 110600 | tf_op jit(solution)/shard_map/ppermute | solution.py:393
  167.2 4.7 %collective-permute-start.6 = (f32[8,1152]{1,0:T(8,128)S(1)}, f32[8,1152]{1,0:T(8,128)S(1)}, u32[]{:S(2)}, u32[]{:S(2)}) collective-permute-start(f32[8,1152]{1,0:T(8,128)S(1)} %add.24), channel_id=1, source_target_pairs={{0,6},{1,7},{2,4},{3,5},{4,2},{5,3},{6,0},{7,1},{8,14},{9,15},{10,... | collective-permute-start | bytes 110600 | tf_op jit(solution)/shard_map/ppermute | solution.py:393
  171.9 5.6 %collective-permute-start.7 = (f32[8,1152]{1,0:T(8,128)S(1)}, f32[8,1152]{1,0:T(8,128)S(1)}, u32[]{:S(2)}, u32[]{:S(2)}) collective-permute-start(f32[8,1152]{1,0:T(8,128)S(1)} %add_add_fusion.mine_ref), channel_id=1, source_target_pairs={{0,1},{1,0},{2,3},{3,2},{4,5},{5,4},{6,7},{7,6},{8,9},{9,8},{10,11... | collective-permute-start | bytes 110600 | tf_op jit(solution)/shard_map/ppermute | solution.py:393
